TPU v7x, 128 devices: a whole 4x4x4 slice. The times are simulated.
128 devices in a mesh: row: 8 (over x, core), col: 16 (over z, y).
Axes of the slice: x: 4, y: 4, z: 4, core: 2. Of those that a mesh axis runs over, the one named last changes fastest.
Arguments:
- tiles: float32 [1024, 64, 64], P(('row', 'col')), may hold values from -6 to 6
- row_kernels: float32 [1024, 64, 64], P(('row', 'col')), may hold values from -0.2 to 1, as said below
- column_resample_kernels: float32 [1024, 64, 64], P(('row', 'col')), may hold values from -0.2 to 1, as said below
- destination: int32 [1024, 1], P(('row', 'col')), may hold values from 0 to 15; in each aligned block of 8 rows (0 to 7, 8 to 15, ...) no two rows name the same one
- row_offset: int32 [1024], P(('row', 'col')), may hold values from 0 to 64
- col_offset: int32 [1024], P(('row', 'col')), may hold values from 0 to 64
- exposure_weight: float32 [1024], P(('row', 'col')), may hold values from 0.2 to 5
- first_filter: float32 [32, 1, 3, 3], replicated, may hold values from -2 to 2
- first_bias: float32 [32], replicated, may hold values from -1.5 to 1.5
- second_filter: float32 [32, 32, 3, 3], replicated, may hold values from -0.375 to 0.375
- second_bias: float32 [32], replicated, may hold values from -1.5 to 1.5
- third_filter: float32 [32, 32, 3, 3], replicated, may hold values from -0.375 to 0.375
- third_bias: float32 [32], replicated, may hold values from -1.5 to 1.5
Outputs:
- features: float32 [32, 1024, 2048], P(None, 'row', 'col')
Inputs may be any that keep to these rules, and one draw needn't show every extreme that they name: Among the tiles of one device at most 1 share a destination, and in every draw some device has exactly 1 tiles for one destination. `row_kernels`: entry (a, b) of a tile's matrix is the Lanczos-3 kernel sinc(x) sinc(x / 3) at x = b - a - s, zero where |x| >= 3, with one shift s of -0.5 to 0.5 for each tile. `column_resample_kernels`: entry (a, b) of a tile's matrix is the Lanczos-3 kernel sinc(x) sinc(x / 3) at x = b - a - s, zero where |x| >= 3, with one shift s of -0.5 to 0.5 for each tile.
All inputs are finite; a program needn't handle non-finite values.
Results may differ from a plain program's by a relative error of at most 0.0003.
Values sent between devices are 32-bit elements; how exact they have to be, the bound alone decides.
A program may use at most 128 MiB of HBM per device.

v0:
```python
import jax
import jax.numpy as jnp
from jax import lax
from jax.sharding import PartitionSpec as P

PS = 128
PATCH_ROWS_LOCAL = 1
SLOTS = 1


def padded_2(cells, sides, width):
    for axis, dim in sides:
        count = lax.axis_size(axis)
        ends = count - 1
        head = lax.slice_in_dim(cells, 0, width, axis=dim)
        tail = lax.slice_in_dim(cells, cells.shape[dim] - width, cells.shape[dim], axis=dim)
        cells = jnp.concatenate(
            [
                lax.ppermute(tail, axis, [(i, (i + 1) % count) for i in range(ends)]),
                cells,
                lax.ppermute(head, axis, [((i + 1) % count, i) for i in range(ends)]),
            ],
            axis=dim,
        )
    return cells


def resample_all(kernel_rows, images, kernel_column_slice):
    middle_activation = jnp.einsum(
        "iab,ibc->iac", kernel_rows, images, precision=lax.Precision.HIGHEST
    )
    return jnp.einsum(
        "wbz,wuz->wbu", middle_activation, kernel_column_slice, precision=lax.Precision.HIGHEST
    )


def valid_conv(field, conv_kernel_matrix, spacing):
    out = lax.conv_general_dilated(
        field[None],
        conv_kernel_matrix,
        (1, 1),
        "VALID",
        rhs_dilation=(spacing, spacing),
        dimension_numbers=("NCHW", "OIHW", "NCHW"),
        precision=lax.Precision.HIGHEST,
    )
    return out[0]


def place_tiles(images, places, weights, height, width):
    side = images.shape[1]
    span = jnp.arange(side, dtype=jnp.int32)
    row_selection = (
        jnp.arange(height, dtype=jnp.int32)[None, None, :]
        == places[:, 0][:, None, None] + span[None, :, None]
    ).astype(jnp.float32)
    col_pick = (
        jnp.arange(width, dtype=jnp.int32)[None, None, :]
        == places[:, 1][:, None, None] + span[None, :, None]
    ).astype(jnp.float32)
    scaled = images * weights[:, None, None]
    spread = jnp.einsum("iab,ibx->iax", scaled, col_pick, precision=lax.Precision.HIGHEST)
    numer = jnp.einsum("iay,iax->yx", row_selection, spread, precision=lax.Precision.HIGHEST)
    row_cover = jnp.sum(row_selection, axis=1) * weights[:, None]
    col_cover = jnp.sum(col_pick, axis=1)
    cover = jnp.dot(row_cover.T, col_cover, precision=lax.Precision.HIGHEST)
    return numer / (1.0 + cover)


def body(
    tiles,
    row_kernels,
    column_resample_kernels,
    destination,
    row_offset,
    col_offset,
    exposure_weight,
    first_filter,
    first_bias,
    second_filter,
    second_bias,
    third_filter,
    third_bias,
):
    n_col = lax.axis_size("col")
    height = PATCH_ROWS_LOCAL * PS
    width = PS
    total = n_col * SLOTS
    target_patch = destination[:, 0]
    onehot = (target_patch[:, None] == jnp.arange(n_col, dtype=jnp.int32)[None, :]).astype(
        jnp.int32
    )
    earlier = jnp.cumsum(onehot, axis=0) - onehot
    rank = jnp.sum(earlier * onehot, axis=1)
    slot = target_patch * SLOTS + rank
    offsets = jnp.stack([row_offset, col_offset], axis=1)

    def pack(values):
        buffer = jnp.zeros((total,) + values.shape[1:], values.dtype)
        return buffer.at[slot].set(values)

    payload = pack(jnp.stack([tiles, row_kernels, column_resample_kernels], axis=1))
    got_data, places, weights = (
        lax.all_to_all(payload, "col", split_axis=0, concat_axis=0, tiled=True),
        lax.all_to_all(pack(offsets), "col", split_axis=0, concat_axis=0, tiled=True),
        lax.all_to_all(pack(exposure_weight), "col", split_axis=0, concat_axis=0, tiled=True),
    )
    images = resample_all(got_data[:, 1], got_data[:, 0], got_data[:, 2])
    coadd = place_tiles(images, places, weights, height, width)
    initial_conv_bias = first_bias[:, None, None]
    second_b = second_bias[:, None, None]
    third_b = third_bias[:, None, None]
    padded = padded_2(coadd[None], (("row", 1), ("col", 2)), 1)
    first = jax.nn.relu(valid_conv(padded, first_filter, 1) + initial_conv_bias)
    padded_first = padded_2(first, (("row", 1), ("col", 2)), 2)
    second = jax.nn.relu(valid_conv(padded_first, second_filter, 2) + second_b)
    padded_second = padded_2(second, (("row", 1), ("col", 2)), 4)
    return valid_conv(padded_second, third_filter, 4) + third_b


def solution(mesh):
    in_specs = (
        P(("row", "col"), None, None),
        P(("row", "col"), None, None),
        P(("row", "col"), None, None),
        P(("row", "col"), None),
        P(("row", "col")),
        P(("row", "col")),
        P(("row", "col")),
        P(),
        P(),
        P(),
        P(),
        P(),
        P(),
    )
    out_specs = P(None, "row", "col")
    return jax.shard_map(body, mesh=mesh, in_specs=in_specs, out_specs=out_specs, check_vma=False)
```

profile of v0, /device:TPU:1, one launch (start us, length us, event | category | flops | bytes accessed | tf_op | source)
XLA Modules:
  0.0 386.8 jit_solution(17442738069062442578)
XLA Ops:
  3.7 8.6 %all-to-all-start.2 = ((f32[16,1,1]{2,1,0:T(1,128)}), f32[16,1,1]{2,1,0:T(1,128)S(1)}, u32[]{:S(2)}, u32[]{:S(2)}) async-start(f32[16,1,1]{2,1,0:T(1,128)} %copy.127), calls=%async_computation.2 | async-start | bytes 16384 | tf_op jit(solution)/shard_map/all_to_all | solution.py:106
  18.7 6.3 %all-to-all-start = ((s32[16,1,2]{2,1,0:T(1,128)}), s32[16,1,2]{2,1,0:T(1,128)S(1)}, u32[]{:S(2)}, u32[]{:S(2)}) async-start(s32[16,1,2]{2,1,0:T(1,128)} %bitcast.35), calls=%async_computation | async-start | bytes 16384 | tf_op jit(solution)/shard_map/all_to_all | solution.py:105
  25.2 6.2 %all-to-all-done = s32[16,1,2]{2,1,0:T(1,128)S(1)} async-done(((s32[16,1,2]{2,1,0:T(1,128)}), s32[16,1,2]{2,1,0:T(1,128)S(1)}, u32[]{:S(2)}, u32[]{:S(2)}) %all-to-all-start) | async-done | bytes 160 | tf_op jit(solution)/shard_map/all_to_all | solution.py:105
  31.4 3.6 all-to-all-start.1
  35.7 11.3 %all-to-all-done.1 = f32[16,1,12288]{2,1,0:T(1,128)S(1)} async-done(((f32[16,1,12288]{2,1,0:T(1,128)}), f32[16,1,12288]{2,1,0:T(1,128)S(1)}, u32[]{:S(2)}, u32[]{:S(2)}) %all-to-all-start.1) | async-done | bytes 786464 | tf_op jit(solution)/shard_map/all_to_all | solution.py:104
  53.9 6.4 %collective-permute-start = (f32[1,1,128]{2,1,0:T(1,128)S(1)}, f32[1,1,128]{2,1,0:T(1,128)S(1)}, u32[]{:S(2)}, u32[]{:S(2)}) collective-permute-start(f32[1,1,128]{2,1,0:T(1,128)S(1)} %get-tuple-element.15), channel_id=1, source_target_pairs={{0,16},{16,32},{32,48},{48,64},{64,80},{80,96},{96,112},{1,17},{17... | collective-permute-start | bytes 1544 | tf_op jit(solution)/shard_map/ppermute | solution.py:19
  62.3 2.9 collective-permute-done.1
  69.1 3.5 collective-permute-done.3
  76.1 30.9 %broadcast_select_fusion.2 = f32[128,8,17,32]{3,1,2,0:T(8,128)} fusion(pred[8,17]{0,1:T(8,128)(4,1)S(1)} %copy-done.11, f32[32,1,3,3]{0,1,3,2:T(1,128)S(1)} %copy-done.10, f32[1,130,8,19]{2,0,3,1:T(1,128)S(1)} %fusion.71), kind=kOutput, calls=%fused_computation.23 | convolution fusion | flops 60719104 | bytes 2308552 | tf_op jit(solution)/shard_map/conv_general_dilated | solution.py:38
  107.0 8.6 %copy.131 = f32[128,8,17,32]{0,3,2,1:T(8,128)} copy(f32[128,8,17,32]{3,1,2,0:T(8,128)} %broadcast_select_fusion.2) | data formatting | bytes 4456448 | tf_op jit(solution)/shard_map/conv_general_dilated | solution.py:38
  122.9 3.9 collective-permute-start.4
  141.6 3.7 collective-permute-done.7
  150.0 9.4 %copy.137 = f32[32,132,1,8,17]{0,3,4,1,2:T(8,128)} copy(f32[32,132,1,8,17]{1,0,4,3,2:T(8,128)} %bitcast.106) | data formatting | bytes 4595712 | tf_op jit(solution)/shard_map/conv_general_dilated | solution.py:38
  161.3 82.6 %broadcast_select_fusion.1 = f32[128,8,17,32]{3,1,2,0:T(8,128)} fusion(pred[8,17]{0,1:T(8,128)(4,1)S(1)} %copy-done.11, f32[32,32,3,3]{1,0,3,2:T(8,128)S(1)} %copy-done, f32[32,132,1,7,4]{0,3,4,1,2:T(8,128)S(1)} %slice.91, f32[32,132,1,8,17]{0,3,4,1,2:T(8,128)} %copy.137), kind=kOutput, calls=%fused_computation.22 | convolution fusion | flops 1927871488 | bytes 5036168 | tf_op jit(solution)/shard_map/conv_general_dilated | solution.py:38
  243.9 8.6 %copy.138 = f32[128,8,17,32]{0,3,2,1:T(8,128)} copy(f32[128,8,17,32]{3,1,2,0:T(8,128)} %broadcast_select_fusion.1) | data formatting | bytes 4456448 | tf_op jit(solution)/shard_map/conv_general_dilated | solution.py:38
  259.9 4.7 %collective-permute-start.8 = (f32[32,4,128]{2,0,1:T(8,128)S(1)}, f32[32,4,128]{2,0,1:T(8,128)S(1)}, u32[]{:S(2)}, u32[]{:S(2)}) collective-permute-start(f32[32,4,128]{2,0,1:T(8,128)S(1)} %copy.139), channel_id=1, source_target_pairs={{0,16},{16,32},{32,48},{48,64},{64,80},{80,96},{96,112},{1,17},{17... | collective-permute-start | bytes 196616 | tf_op jit(solution)/shard_map/ppermute | solution.py:19
  269.1 2.9 copy.141
  276.9 5.4 %collective-permute-start.10 = (f32[32,136,4]{1,0,2:T(8,128)S(1)}, f32[32,136,4]{1,0,2:T(8,128)S(1)}, u32[]{:S(2)}, u32[]{:S(2)}) collective-permute-start(f32[32,136,4]{1,0,2:T(8,128)S(1)} %get-tuple-element.5), channel_id=1, source_target_pairs={{0,1},{1,2},{2,3},{3,4},{4,5},{5,6},{6,7},{7,8},{8,9},{9,10},{10,1... | collective-permute-start | bytes 208904 | tf_op jit(solution)/shard_map/ppermute | solution.py:19
  284.2 3.8 collective-permute-done.11
  288.0 3.5 pad_maximum_fusion
  291.5 8.3 %copy.144 = f32[32,136,1,8,17]{0,3,4,1,2:T(8,128)} copy(f32[32,136,1,8,17]{1,0,4,3,2:T(8,128)} %bitcast.107) | data formatting | bytes 4734976 | tf_op jit(solution)/shard_map/conv_general_dilated | solution.py:38
  302.7 71.5 %broadcast_select_fusion = f32[128,8,17,32]{3,1,2,0:T(8,128)} fusion(pred[8,17]{0,1:T(8,128)(4,1)S(1)} %copy-done.11, f32[32,32,3,3]{1,0,3,2:T(8,128)S(1)} %copy-done.9, f32[32,136,1,7,8]{0,3,4,1,2:T(8,128)S(1)} %slice.95, f32[32,136,1,8,17]{0,3,4,1,2:T(8,128)} %copy.144), kind=kOutput, calls=%fused_computation.21 | convolution fusion | flops 1928353792 | bytes 5607560 | tf_op jit(solution)/shard_map/conv_general_dilated | solution.py:38
  374.1 7.8 %copy.145 = f32[128,8,17,32]{0,3,2,1:T(8,128)S(1)} copy(f32[128,8,17,32]{3,1,2,0:T(8,128)} %broadcast_select_fusion) | data formatting | bytes 4456448 | tf_op jit(solution)/shard_map/conv_general_dilated | solution.py:38
  383.7 3.0 copy.146
  (96 shorter events, 78.8 us)
Async XLA Ops:
  0.0 161.3 %copy-start = (f32[32,32,3,3]{1,0,3,2:T(8,128)S(1)}, f32[32,32,3,3]{1,0,3,2:T(8,128)}, u32[]{:S(2)}) copy-start(f32[32,32,3,3]{1,0,3,2:T(8,128)} %param.22) | copy-start | bytes 110596
  3.7 15.0 %all-to-all-start.2 = ((f32[16,1,1]{2,1,0:T(1,128)}), f32[16,1,1]{2,1,0:T(1,128)S(1)}, u32[]{:S(2)}, u32[]{:S(2)}) async-start(f32[16,1,1]{2,1,0:T(1,128)} %copy.127), calls=%async_computation.2 | async-start | bytes 16384 | tf_op jit(solution)/shard_map/all_to_all | solution.py:106
  18.7 12.7 %all-to-all-start = ((s32[16,1,2]{2,1,0:T(1,128)}), s32[16,1,2]{2,1,0:T(1,128)S(1)}, u32[]{:S(2)}, u32[]{:S(2)}) async-start(s32[16,1,2]{2,1,0:T(1,128)} %bitcast.35), calls=%async_computation | async-start | bytes 16384 | tf_op jit(solution)/shard_map/all_to_all | solution.py:105
  31.4 15.6 %all-to-all-start.1 = ((f32[16,1,12288]{2,1,0:T(1,128)}), f32[16,1,12288]{2,1,0:T(1,128)S(1)}, u32[]{:S(2)}, u32[]{:S(2)}) async-start(f32[16,1,12288]{2,1,0:T(1,128)} %reshape.133), calls=%async_computation.1 | async-start | bytes 1572864 | tf_op jit(solution)/shard_map/all_to_all | solution.py:104
  53.9 8.4 %collective-permute-start = (f32[1,1,128]{2,1,0:T(1,128)S(1)}, f32[1,1,128]{2,1,0:T(1,128)S(1)}, u32[]{:S(2)}, u32[]{:S(2)}) collective-permute-start(f32[1,1,128]{2,1,0:T(1,128)S(1)} %get-tuple-element.15), channel_id=1, source_target_pairs={{0,16},{16,32},{32,48},{48,64},{64,80},{80,96},{96,112},{1,17},{17... | collective-permute-start | bytes 1544 | tf_op jit(solution)/shard_map/ppermute | solution.py:19
  60.3 4.9 %collective-permute-start.1 = (f32[1,1,128]{2,1,0:T(1,128)S(1)}, f32[1,1,128]{2,1,0:T(1,128)S(1)}, u32[]{:S(2)}, u32[]{:S(2)}) collective-permute-start(f32[1,1,128]{2,1,0:T(1,128)S(1)} %get-tuple-element.16), channel_id=1, source_target_pairs={{16,0},{32,16},{48,32},{64,48},{80,64},{96,80},{112,96},{17,1},{33... | collective-permute-start | bytes 1544 | tf_op jit(solution)/shard_map/ppermute | solution.py:21
  65.3 3.8 collective-permute-start.2
  67.5 5.1 %collective-permute-start.3 = (f32[1,130,1]{2,1,0:T(8,128)S(1)}, f32[1,130,1]{2,1,0:T(8,128)S(1)}, u32[]{:S(2)}, u32[]{:S(2)}) collective-permute-start(f32[1,130,1]{2,1,0:T(8,128)S(1)} %get-tuple-element.14), channel_id=1, source_target_pairs={{1,0},{2,1},{3,2},{4,3},{5,4},{6,5},{7,6},{8,7},{9,8},{10,9},{11,1... | collective-permute-start | bytes 1568 | tf_op jit(solution)/shard_map/ppermute | solution.py:21
  107.0 8.6 %copy-start.6 = (f32[32]{0:T(128)S(1)}, f32[32]{0:T(128)}, u32[]{:S(2)}) copy-start(f32[32]{0:T(128)} %param.21) | copy-start | bytes 388
  122.9 8.4 %collective-permute-start.4 = (f32[32,2,128]{2,0,1:T(8,128)S(1)}, f32[32,2,128]{2,0,1:T(8,128)S(1)}, u32[]{:S(2)}, u32[]{:S(2)}) collective-permute-start(f32[32,2,128]{2,0,1:T(8,128)S(1)} %copy.132), channel_id=1, source_target_pairs={{0,16},{16,32},{32,48},{48,64},{64,80},{80,96},{96,112},{1,17},{17... | collective-permute-start | bytes 98312 | tf_op jit(solution)/shard_map/ppermute | solution.py:19
  129.5 5.2 %collective-permute-start.5 = (f32[32,2,128]{2,0,1:T(8,128)S(1)}, f32[32,2,128]{2,0,1:T(8,128)S(1)}, u32[]{:S(2)}, u32[]{:S(2)}) collective-permute-start(f32[32,2,128]{2,0,1:T(8,128)S(1)} %copy.133), channel_id=1, source_target_pairs={{16,0},{32,16},{48,32},{64,48},{80,64},{96,80},{112,96},{17,1},{33... | collective-permute-start | bytes 98312 | tf_op jit(solution)/shard_map/ppermute | solution.py:21
  137.5 7.8 %copy-start.2 = (f32[32,2,128]{1,0,2:T(8,128)S(1)}, f32[32,2,128]{1,0,2:T(8,128)}, u32[]{:S(2)}) copy-start(f32[32,2,128]{1,0,2:T(8,128)} %copy.134) | copy-start | bytes 98308
  137.5 7.8 %copy-start.4 = (f32[32,2,128]{1,0,2:T(8,128)S(1)}, f32[32,2,128]{1,0,2:T(8,128)}, u32[]{:S(2)}) copy-start(f32[32,2,128]{1,0,2:T(8,128)} %copy.135) | copy-start | bytes 98308
  138.6 3.0 collective-permute-start.6
  140.3 5.0 %collective-permute-start.7 = (f32[32,132,2]{1,0,2:T(8,128)S(1)}, f32[32,132,2]{1,0,2:T(8,128)S(1)}, u32[]{:S(2)}, u32[]{:S(2)}) collective-permute-start(f32[32,132,2]{1,0,2:T(8,128)S(1)} %get-tuple-element.8), channel_id=1, source_target_pairs={{1,0},{2,1},{3,2},{4,3},{5,4},{6,5},{7,6},{8,7},{9,8},{10,9},{11,1... | collective-permute-start | bytes 101384 | tf_op jit(solution)/shard_map/ppermute | solution.py:21
  243.9 8.6 %copy-start.7 = (f32[32]{0:T(128)S(1)}, f32[32]{0:T(128)}, u32[]{:S(2)}) copy-start(f32[32]{0:T(128)} %param.23) | copy-start | bytes 388
  259.9 9.2 %collective-permute-start.8 = (f32[32,4,128]{2,0,1:T(8,128)S(1)}, f32[32,4,128]{2,0,1:T(8,128)S(1)}, u32[]{:S(2)}, u32[]{:S(2)}) collective-permute-start(f32[32,4,128]{2,0,1:T(8,128)S(1)} %copy.139), channel_id=1, source_target_pairs={{0,16},{16,32},{32,48},{48,64},{64,80},{80,96},{96,112},{1,17},{17... | collective-permute-start | bytes 196616 | tf_op jit(solution)/shard_map/ppermute | solution.py:19
  267.2 5.6 %collective-permute-start.9 = (f32[32,4,128]{2,0,1:T(8,128)S(1)}, f32[32,4,128]{2,0,1:T(8,128)S(1)}, u32[]{:S(2)}, u32[]{:S(2)}) collective-permute-start(f32[32,4,128]{2,0,1:T(8,128)S(1)} %copy.140), channel_id=1, source_target_pairs={{16,0},{32,16},{48,32},{64,48},{80,64},{96,80},{112,96},{17,1},{33... | collective-permute-start | bytes 196616 | tf_op jit(solution)/shard_map/ppermute | solution.py:21
  275.6 12.3 %copy-start.3 = (f32[32,4,128]{1,0,2:T(8,128)S(1)}, f32[32,4,128]{1,0,2:T(8,128)}, u32[]{:S(2)}) copy-start(f32[32,4,128]{1,0,2:T(8,128)} %copy.141) | copy-start | bytes 196612
  275.6 12.3 %copy-start.5 = (f32[32,4,128]{1,0,2:T(8,128)S(1)}, f32[32,4,128]{1,0,2:T(8,128)}, u32[]{:S(2)}) copy-start(f32[32,4,128]{1,0,2:T(8,128)} %copy.142) | copy-start | bytes 196612
  276.9 7.3 %collective-permute-start.10 = (f32[32,136,4]{1,0,2:T(8,128)S(1)}, f32[32,136,4]{1,0,2:T(8,128)S(1)}, u32[]{:S(2)}, u32[]{:S(2)}) collective-permute-start(f32[32,136,4]{1,0,2:T(8,128)S(1)} %get-tuple-element.5), channel_id=1, source_target_pairs={{0,1},{1,2},{2,3},{3,4},{4,5},{5,6},{6,7},{7,8},{8,9},{9,10},{10,1... | collective-permute-start | bytes 208904 | tf_op jit(solution)/shard_map/ppermute | solution.py:19
  282.2 5.7 %collective-permute-start.11 = (f32[32,136,4]{1,0,2:T(8,128)S(1)}, f32[32,136,4]{1,0,2:T(8,128)S(1)}, u32[]{:S(2)}, u32[]{:S(2)}) collective-permute-start(f32[32,136,4]{1,0,2:T(8,128)S(1)} %get-tuple-element.6), channel_id=1, source_target_pairs={{1,0},{2,1},{3,2},{4,3},{5,4},{6,5},{7,6},{8,7},{9,8},{10,9},{11,1... | collective-permute-start | bytes 208904 | tf_op jit(solution)/shard_map/ppermute | solution.py:21
  374.1 7.8 %copy-start.8 = (f32[32]{0:T(128)S(1)}, f32[32]{0:T(128)}, u32[]{:S(2)}) copy-start(f32[32]{0:T(128)} %param.25) | copy-start | bytes 388
  382.0 4.6 %copy-start.1 = (f32[32,32,3,3]{1,0,3,2:T(8,128)S(1)}, f32[32,32,3,3]{1,0,3,2:T(8,128)}, u32[]{:S(2)}) copy-start(f32[32,32,3,3]{1,0,3,2:T(8,128)} %param.22) | copy-start | bytes 110596
  (3 other events, 9.4 us)
where the time goes:
time: 392 us; the launch traced here: 387 us
  matrix products  188 us (48%)
  local copies, waits for them, and re-layouts  89.6 us (23%)
  starting transfers between devices  52.5 us (13%)
  waiting for transfers between devices  33.6 us (9%)
  other arithmetic  22.2 us (6%)
    conv_general_dilated x3, matrix products, valid_conv(): lax.conv_general_dilated(field[None], conv_kernel_matrix, (1, 1), 'VALID'...  185 us
    conv_general_dilated x9, local copies, waits for them, and re-layouts, valid_conv(): lax.conv_general_dilated(field[None], conv_kernel_matrix, (1, 1), 'VALID'...  49.3 us
    ppermute x6, starting transfers between devices, padded_2(): lax.ppermute(tail, axis, [(i, (i + 1) % count) for i in range(ends)])  24.2 us
    ppermute x6, waiting for transfers between devices, padded_2(): lax.ppermute(head, axis, [((i + 1) % count, i) for i in range(ends)])  15.1 us
    all_to_all x1, waiting for transfers between devices, body(): lax.all_to_all(payload, 'col', split_axis=0, concat_axis=0, tiled=True)  11.3 us
    slice x6, local copies, waits for them, and re-layouts, padded_2(): lax.slice_in_dim(cells, cells.shape[dim] - width, cells.shape[dim], axis=...  10.9 us
    ppermute x6, starting transfers between devices, padded_2(): lax.ppermute(head, axis, [((i + 1) % count, i) for i in range(ends)])  9.87 us
    all_to_all x1, starting transfers between devices, body(): lax.all_to_all(pack(exposure_weight), 'col', split_axis=0, concat_axis=0,...  8.6 us
  transfers between devices with their start and end apart: 15, of which 10 were waited for; matrix products, arithmetic and copies ran while one was open for 5% of the time, Pallas kernels for 0%

commit v1 on v0

v1 whole, which is shorter than its diff:
```python
import functools
import jax
import jax.numpy as jnp
from jax import lax
from jax.experimental import pallas as pl
from jax.experimental.pallas import tpu as pltpu
from jax.sharding import PartitionSpec as P

BF = jnp.bfloat16
F32 = jnp.float32


def split(x):
    hi = x.astype(BF)
    return hi, (x - hi.astype(F32)).astype(BF)


def build_weights(f1_ref, b1_ref, f2_ref, f3_ref, w1_ref, w2_ref, w3_ref):
    for f_ref, w_ref in ((f2_ref, w2_ref), (f3_ref, w3_ref)):
        for dx in range(3):
            row = jnp.concatenate(
                [f_ref[dy * 3 + dx] for dy in range(3)] + [jnp.zeros((32, 160), F32)], axis=1)
            for yo in range(6):
                moved = row if yo == 0 else pltpu.roll(row, 32 * yo, 1)
                hi, lo = split(moved)
                w_ref[0, dx, yo * 32:(yo + 1) * 32, :] = hi
                w_ref[1, dx, yo * 32:(yo + 1) * 32, :] = lo
    f1 = f1_ref[...]
    hi, lo = split(f1)
    hi = hi.astype(F32)
    lo = lo.astype(F32)
    b = b1_ref[...]
    bhi, blo = split(b)
    lane = lax.broadcasted_iota(jnp.int32, (32, 256), 1)
    for yo in range(8):
        acc = jnp.where(lane == 144, bhi.astype(F32), 0.0) + jnp.where(lane == 145, blo.astype(F32), 0.0)
        for part, w in enumerate((hi, hi, lo)):
            for dx in range(3):
                for dy in range(3):
                    acc = acc + jnp.where(lane == part * 48 + dx * 16 + yo + dy, w[:, dy * 3 + dx:dy * 3 + dx + 1], 0.0)
        r = (yo % 2) * 128 + (yo // 2) * 32
        w1_ref[r:r + 32, :] = acc.astype(BF)


def conv_body(row, col, p_ref, w1_ref, w2_ref, w3_ref, b2_ref, b3_ref, out_ref,
              ps, f_hi, f_lo, s_hi, s_lo):
    p = p_ref[...]
    ps[0] = pltpu.roll(p, 1, 1)
    ps[1] = p
    ps[2] = pltpu.roll(p, 255, 1)
    lane = lax.broadcasted_iota(jnp.int32, (1, 256), 1)
    dead = jnp.logical_or(jnp.logical_and(col == 0, lane >= 192),
                          jnp.logical_and(col == 15, jnp.logical_and(lane >= 128, lane < 192)))
    cmask = jnp.where(dead, 0.0, 1.0)
    sub = lax.broadcasted_iota(jnp.int32, (16, 256), 0)
    ones = jnp.where(sub < 2, 1.0, 0.0).astype(BF)
    pad = jnp.zeros((96, 256), BF)
    w1 = w1_ref[...]
    n_rows = 1024
    base = row * 128

    def valid(y):
        yy = base + y
        return jnp.where(jnp.logical_and(yy >= 0, yy < n_rows), 1.0, 0.0)

    @pl.loop(0, 18)
    def _(g):
        hs, ls = [], []
        for dx in range(3):
            h, l = split(ps[dx, pl.ds(pl.multiple_of(8 * g, 8), 16), :])
            hs.append(h)
            ls.append(l)
        rhs = jnp.concatenate(hs + ls + hs + [ones, pad], axis=0)
        acc = jnp.dot(w1, rhs, preferred_element_type=F32)
        for q in range(2):
            for m in range(4):
                mask = cmask * valid(8 * g + 2 * m + q - 6)
                v = jnp.maximum(acc[q * 128 + m * 32:q * 128 + m * 32 + 32, :], 0.0) * mask
                h, l = split(v)
                at = pl.ds(pl.multiple_of((4 * g + m) * 32, 32), 32)
                f_hi[q, at, :] = h
                f_lo[q, at, :] = l

    b2 = b2_ref[...]

    @pl.loop(0, 24)
    def _(t):
        q = lax.rem(t, 2)
        m0 = jnp.minimum(6 * (t // 2), 62)
        at = pl.ds(pl.multiple_of(32 * m0, 64), 256)
        hi = f_hi[q, at, :]
        lo = f_lo[q, at, :]
        parts = []
        for dx in range(3):
            parts.append(jnp.dot(w2_ref[0, dx], hi, preferred_element_type=F32)
                         + jnp.dot(w2_ref[1, dx], hi, preferred_element_type=F32)
                         + jnp.dot(w2_ref[0, dx], lo, preferred_element_type=F32))
        acc = parts[1] + pltpu.roll(parts[0], 2, 1) + pltpu.roll(parts[2], 254, 1)
        n0 = m0 // 2
        for yo in range(6):
            mask = cmask * valid(2 * (m0 + yo) + q - 4)
            v = acc[yo * 32:yo * 32 + 32, :]
            v = jnp.maximum(v + b2, 0.0) * mask
            r = 2 * (yo % 2) + q
            at = pl.ds(pl.multiple_of((n0 + yo // 2) * 32, 32), 32)
            for k, sh in enumerate((pltpu.roll(v, 4, 1), v, pltpu.roll(v, 252, 1))):
                h, l = split(sh[:, :128])
                s_hi[k, r, at, :] = h
                s_lo[k, r, at, :] = l

    b3 = b3_ref[...][:, :128]

    @pl.loop(0, 12)
    def _(t):
        half = lax.rem(t, 2)
        n0 = jnp.minimum(6 * (t // 2), 26)
        at = pl.ds(pl.multiple_of(32 * n0, 64), 256)
        acc = None
        for dx in range(3):
            hi = jnp.concatenate([s_hi[dx, 2 * half, at, :], s_hi[dx, 2 * half + 1, at, :]], axis=1)
            lo = jnp.concatenate([s_lo[dx, 2 * half, at, :], s_lo[dx, 2 * half + 1, at, :]], axis=1)
            part = (jnp.dot(w3_ref[0, dx], hi, preferred_element_type=F32)
                    + jnp.dot(w3_ref[1, dx], hi, preferred_element_type=F32)
                    + jnp.dot(w3_ref[0, dx], lo, preferred_element_type=F32))
            acc = part if acc is None else acc + part
        for e in range(2):
            for yo in range(6):
                v = acc[yo * 32:yo * 32 + 32, e * 128:e * 128 + 128] + b3
                y = 4 * (n0 + yo) + 2 * half + e
                for k in range(4):
                    out_ref[pl.ds(k * 1024 + y, 8, stride=128), :] = v[8 * k:8 * k + 8, :]


def conv_kernel(*refs):
    conv_body(lax.axis_index("row"), lax.axis_index("col"), *refs)


W_SHAPES = [jax.ShapeDtypeStruct((256, 256), BF), jax.ShapeDtypeStruct((2, 3, 192, 256), BF),
            jax.ShapeDtypeStruct((2, 3, 192, 256), BF)]


def conv_call(p, w1, w2, w3, b2, b3):
    vm = pl.BlockSpec(memory_space=pltpu.VMEM)
    return pl.pallas_call(
        conv_kernel,
        out_shape=jax.ShapeDtypeStruct((4096, 128), F32),
        in_specs=[vm] * 6,
        out_specs=vm,
        scratch_shapes=[pltpu.VMEM((3, 152, 256), F32),
                        pltpu.VMEM((2, 74 * 32, 256), BF), pltpu.VMEM((2, 74 * 32, 256), BF),
                        pltpu.VMEM((3, 4, 34 * 32, 128), BF), pltpu.VMEM((3, 4, 34 * 32, 128), BF)],
        compiler_params=pltpu.CompilerParams(vmem_limit_bytes=48 << 20),
        name="convs",
    )(p, w1, w2, w3, b2, b3)


N_ROW = 8
N_COL = 16
TILES_DEV = 8
TS = 64
MESH = pl.DeviceIdType.MESH


def dot3(ah, al, bh, bl, dims):
    d = functools.partial(lax.dot_general, dimension_numbers=(dims, ((), ())), preferred_element_type=F32)
    return d(ah, bh) + d(al, bh) + d(ah, bl)


def comm_kernel(dest, roff, coff, wgt, tiles, rker, cker, f1_ref, b1_ref, f2_ref, f3_ref,
                p_ref, w1_ref, w2_ref, w3_ref,
                ckpad, packed, send, recv, spread, edge_out, edge_in,
                send_sem, recv_sem, esend_sem, erecv_sem):
    row = lax.axis_index("row")
    col = lax.axis_index("col")
    up = lax.rem(row + N_ROW - 1, N_ROW)
    down = lax.rem(row + 1, N_ROW)
    left = lax.rem(col + N_COL - 1, N_COL)
    right = lax.rem(col + 1, N_COL)

    barrier = pltpu.get_barrier_semaphore()

    @pl.loop(1, N_COL)
    def _(k):
        pl.semaphore_signal(barrier, inc=1, device_id=(row, lax.rem(col + k, N_COL)), device_id_type=MESH)

    for r in (up, down):
        for c in (left, col, right):
            pl.semaphore_signal(barrier, inc=1, device_id=(r, c), device_id_type=MESH)

    ckpad[...] = jnp.zeros_like(ckpad)

    @pl.loop(0, TILES_DEV)
    def _(t):
        rh, rl = split(rker[t])
        th, tl = split(tiles[t])
        mid = dot3(rh, rl, th, tl, ((1,), (0,)))
        ckpad[TS:2 * TS, :] = cker[t]
        placed = ckpad[pl.ds(TS - coff[t], 2 * TS), :]
        mh, ml = split(mid)
        ch, cl = split(placed)
        img = dot3(mh, ml, ch, cl, ((1,), (1,)))
        packed[t] = img[:32, :] + pltpu.roll(img[32:, :], 64, 1)

    sub8 = lax.broadcasted_iota(jnp.int32, (8, 128), 0)

    @pl.loop(0, N_COL)
    def _(c):
        acc = None
        ro = jnp.float32(0.0)
        co = jnp.float32(0.0)
        w = jnp.float32(0.0)
        for t in range(TILES_DEV):
            hit = jnp.where(dest[t] == c, 1.0, 0.0)
            wt = hit * wgt[t]
            ro = ro + hit * roff[t].astype(F32)
            co = co + hit * coff[t].astype(F32)
            w = w + wt
            term = packed[t] * wt
            acc = term if acc is None else acc + term
        send[c, 0:32, :] = acc
        send[c, 32:40, :] = jnp.where(sub8 == 0, ro, jnp.where(sub8 == 1, co, w))

    pl.semaphore_wait(barrier, N_COL - 1 + 6)

    def tile_copy(k):
        c = lax.rem(col + k, N_COL)
        return pltpu.make_async_remote_copy(
            src_ref=send.at[c], dst_ref=recv.at[k], send_sem=send_sem.at[k], recv_sem=recv_sem.at[k],
            device_id=(row, c), device_id_type=MESH)

    @pl.loop(1, N_COL)
    def _(k):
        tile_copy(k).start()

    recv[0] = send[col]
    build_weights(f1_ref, b1_ref, f2_ref, f3_ref, w1_ref, w2_ref, w3_ref)

    @pl.loop(1, N_COL)
    def _(k):
        tile_copy(k).wait()

    lane = lax.broadcasted_iota(jnp.int32, (1, 128), 1).astype(F32)
    suby = lax.broadcasted_iota(jnp.int32, (128, 128), 0).astype(F32)
    lanes = lax.broadcasted_iota(jnp.int32, (128, 128), 1)
    lane_a = (lanes % TS).astype(F32)
    cover = jnp.zeros((128, 128), F32)
    numer = jnp.zeros((128, 256), F32)
    for pair in range(N_COL // 2):
        ros = []
        for e in range(2):
            s = 2 * pair + e
            pk = recv[s, 0:32, :]
            ro = recv[s, 32:33, :]
            co = recv[s, 33:34, :]
            w = recv[s, 34:35, :]
            at = lane - co
            inside = jnp.logical_and(at >= 0.0, at < float(TS))
            a = jnp.where(inside, pk, 0.0)
            b = jnp.where(inside, pltpu.roll(pk, 64, 1), 0.0)
            for half, v in enumerate((a, b)):
                h, l = split(v)
                r = s * TS + half * 32
                spread[r:r + 32, 0:128] = h
                spread[r:r + 32, 128:256] = l
            wcol = jnp.where(inside, w, 0.0)
            dy = suby - ro
            cover = cover + jnp.where(jnp.logical_and(dy >= 0.0, dy < float(TS)), wcol, 0.0)
            ros.append(ro)
        want = jnp.where(lanes < TS, ros[0], ros[1]) + lane_a
        pick = jnp.where(suby == want, 1.0, 0.0).astype(BF)
        numer = numer + jnp.dot(pick, spread[pair * 128:pair * 128 + 128, :], preferred_element_type=F32)
    coadd = (numer[:, :128] + numer[:, 128:]) / (1.0 + cover)

    edge_out[0] = coadd[0:8, :]
    edge_out[1] = coadd[120:128, :]
    lane8 = lax.broadcasted_iota(jnp.int32, (8, 128), 1)
    lcols = jnp.zeros((8, 128), F32)
    rcols = jnp.zeros((8, 128), F32)
    for k in range(16):
        blk = coadd[8 * k:8 * k + 8, :]
        here = jnp.logical_and(lane8 >= 8 * k, lane8 < 8 * k + 8)
        lcols = jnp.where(here, blk if k == 0 else pltpu.roll(blk, 8 * k, 1), lcols)
        rcols = jnp.where(here, blk if k == 15 else pltpu.roll(blk, 8 * k + 8, 1), rcols)
    edge_out[2] = lcols
    edge_out[3] = rcols
    plan = ((0, 1, (down, col)), (1, 0, (up, col)), (2, 3, (row, right)), (3, 2, (row, left)),
            (4, 1, (down, right)), (5, 1, (down, left)), (6, 0, (up, right)), (7, 0, (up, left)))
    copies = [pltpu.make_async_remote_copy(
        src_ref=edge_out.at[src], dst_ref=edge_in.at[slot], send_sem=esend_sem.at[slot],
        recv_sem=erecv_sem.at[slot], device_id=dev, device_id_type=MESH) for slot, src, dev in plan]
    for c in copies:
        c.start()
    p_ref[...] = jnp.zeros_like(p_ref)
    p_ref[7:135, 0:128] = coadd
    for c in copies:
        c.wait()

    has_up = jnp.where(row > 0, 1.0, 0.0)
    has_down = jnp.where(row < N_ROW - 1, 1.0, 0.0)
    has_left = jnp.where(col > 0, 1.0, 0.0)
    has_right = jnp.where(col < N_COL - 1, 1.0, 0.0)
    side = jnp.where(lane8 < TS, has_right, has_left)
    p_ref[0:7, 0:128] = edge_in[0][1:8, :] * has_up
    p_ref[135:142, 0:128] = edge_in[1][0:7, :] * has_down
    p_ref[0:7, 128:256] = (jnp.where(lane8 < TS, edge_in[5], edge_in[4]) * side * has_up)[1:8, :]
    p_ref[135:142, 128:256] = (jnp.where(lane8 < TS, edge_in[7], edge_in[6]) * side * has_down)[0:7, :]
    from_left = edge_in[2]
    from_right = edge_in[3]
    for k in range(16):
        r = from_right if k == 0 else pltpu.roll(from_right, 128 - 8 * k, 1)
        l = from_left if k == 15 else pltpu.roll(from_left, 120 - 8 * k, 1)
        p_ref[7 + 8 * k:15 + 8 * k, 128:256] = jnp.where(lane8 < TS, r, l) * side


def comm_call(dest, roff, coff, wgt, tiles, rker, cker, f1, b1, f2, f3):
    vm = pl.BlockSpec(memory_space=pltpu.VMEM)
    sm = pl.BlockSpec(memory_space=pltpu.SMEM)
    return pl.pallas_call(
        comm_kernel,
        out_shape=[jax.ShapeDtypeStruct((152, 256), F32)] + W_SHAPES,
        in_specs=[sm] * 4 + [vm] * 7,
        out_specs=[vm] * 4,
        scratch_shapes=[
            pltpu.VMEM((3 * TS, TS), F32),
            pltpu.VMEM((TILES_DEV, 32, 128), F32),
            pltpu.VMEM((N_COL, 40, 128), F32),
            pltpu.VMEM((N_COL, 40, 128), F32),
            pltpu.VMEM((N_COL * TS, 256), BF),
            pltpu.VMEM((4, 8, 128), F32),
            pltpu.VMEM((8, 8, 128), F32),
            pltpu.SemaphoreType.DMA((N_COL,)),
            pltpu.SemaphoreType.DMA((N_COL,)),
            pltpu.SemaphoreType.DMA((8,)),
            pltpu.SemaphoreType.DMA((8,)),
        ],
        compiler_params=pltpu.CompilerParams(collective_id=0, has_side_effects=True, vmem_limit_bytes=32 << 20),
        name="coadd",
    )(dest, roff, coff, wgt, tiles, rker, cker, f1, b1, f2, f3)


def body(tiles, row_kernels, column_resample_kernels, destination, row_offset, col_offset, exposure_weight,
         first_filter, first_bias, second_filter, second_bias, third_filter, third_bias):
    taps = lambda f: jnp.transpose(f, (2, 3, 0, 1)).reshape(9, 32, 32)
    wide = lambda b: jnp.broadcast_to(b[:, None], (32, 256))
    p, w1, w2, w3 = comm_call(destination[:, 0], row_offset, col_offset, exposure_weight, tiles, row_kernels,
                              column_resample_kernels, first_filter.reshape(32, 9), first_bias[:, None],
                              taps(second_filter), taps(third_filter))
    out = conv_call(p, w1, w2, w3, wide(second_bias), wide(third_bias))
    return out.reshape(32, 128, 128)


def solution(mesh):
    held = P(("row", "col"))
    in_specs = (held,) * 7 + (P(),) * 6
    return jax.shard_map(body, mesh=mesh, in_specs=in_specs, out_specs=P(None, "row", "col"), check_vma=False)
```

time: 392 us -> 58.9 us (0.15); the launches traced: 387 us -> 58.6 us
  matrix products: 188 us -> 0 us
  local copies, waits for them, and re-layouts: 89.6 us -> 9.57 us
  starting transfers between devices: 52.5 us -> 0 us
  Pallas kernels: 0 us -> 48.3 us
  waiting for transfers between devices: 33.6 us -> 0 us
  other arithmetic: 22.2 us -> 0.71 us
    conv_general_dilated x3 -> x0, matrix products: 185 us -> none  [valid_conv(): lax.conv_general_dilated(field[None], conv_kernel_matrix, (1, 1), 'VALID'...]
    conv_general_dilated x9 -> x0, local copies, waits for them, and re-layouts: 49.3 us -> none  [valid_conv(): lax.conv_general_dilated(field[None], conv_kernel_matrix, (1, 1), 'VALID'...]
    pallas_call x0 -> x2, Pallas kernels: none -> 48.3 us  [the longest x1 26.6 us: conv_call(): pl.pallas_call(conv_kernel, out_shape=jax.ShapeDtypeStruct((4096, 128), F...]
    ppermute x12 -> x0, starting transfers between devices: 34 us -> none  [the longest x6 24.2 us: padded_2(): lax.ppermute(tail, axis, [(i, (i + 1) % count) for i in range(ends)])]
    all_to_all x3 -> x0, starting transfers between devices: 18.5 us -> none  [the longest x1 8.6 us: body(): lax.all_to_all(pack(exposure_weight), 'col', split_axis=0, concat_axis=0,...]
    all_to_all x3 -> x0, waiting for transfers between devices: 17.9 us -> none  [the longest x1 11.3 us: body(): lax.all_to_all(payload, 'col', split_axis=0, concat_axis=0, tiled=True)]
    slice x9 -> x0, local copies, waits for them, and re-layouts: 16.3 us -> none  [the longest x6 10.9 us: padded_2(): lax.slice_in_dim(cells, cells.shape[dim] - width, cells.shape[dim], axis=...]
    ppermute x12 -> x0, waiting for transfers between devices: 15.7 us -> none  [the longest x6 15.1 us: padded_2(): lax.ppermute(head, axis, [((i + 1) % count, i) for i in range(ends)])]
  transfers between devices with their start and end apart: 15 -> 0, of which waited for: 10 -> 0; matrix products, arithmetic and copies ran while one was open for 5% -> 0% of each run, Pallas kernels for 0% -> 0%
where the time goes in v1:
time: 58.9 us; the launch traced here: 58.6 us
  Pallas kernels  48.3 us (82%)
  local copies, waits for them, and re-layouts  9.57 us (16%)
  other arithmetic  0.71 us (1%)
    pallas_call x1, Pallas kernels, conv_call(): pl.pallas_call(conv_kernel, out_shape=jax.ShapeDtypeStruct((4096, 128), F...  26.6 us
    pallas_call x1, Pallas kernels, comm_call(): pl.pallas_call(comm_kernel, out_shape=[jax.ShapeDtypeStruct((152, 256), F...  21.7 us
    unnamed x18, local copies, waits for them, and re-layouts  7.29 us
    broadcast_in_dim x2, local copies, waits for them, and re-layouts, body(): wide = lambda b: jnp.broadcast_to(b[:, None], (32, 256))  1.45 us

profile of v1, /device:TPU:1, one launch (start us, length us, event | category | flops | bytes accessed | tf_op | source)
XLA Modules:
  0.0 58.6 jit_solution(8241012274787991869)
XLA Ops:
  0.0 0.7 %reduce = f32[32,3,3]{0,2,1:T(4,128)S(1)} reduce(f32[32,1,3,3]{0,1,3,2:T(1,128)} %param.20, f32[]{:T(128)} %constant.7), dimensions={1}, to_apply=%param.20.reduce_sub_computation | reduce | bytes 2308 | tf_op args[7]
  0.7 0.1 copy.16.f1_ref
  0.8 0.7 %copy.17.b1_ref = f32[32,1]{1,0:T(8,128)S(1)} copy(f32[32,1]{0,1:T(1,128)} %bitcast.14) | data formatting | bytes 256 | tf_op jit(solution)/shard_map/broadcast_in_dim | solution.py:346
  1.6 0.7 %broadcast_in_dim.7.refs_4_ = f32[32,256]{1,0:T(8,128)S(1)} broadcast(f32[32]{0:T(128)} %param.23), dimensions={0} | broadcast | bytes 32896 | tf_op jit(solution)/shard_map/broadcast_in_dim | solution.py:344
  2.3 0.7 %broadcast_in_dim.8.refs_5_ = f32[32,256]{1,0:T(8,128)S(1)} broadcast(f32[32]{0:T(128)} %param.25), dimensions={0} | broadcast | bytes 32896 | tf_op jit(solution)/shard_map/broadcast_in_dim | solution.py:344
  3.0 0.0 copy-start
  3.0 0.9 %copy-done = f32[8,64,64]{2,1,0:T(8,128)S(1)} copy-done((f32[8,64,64]{2,1,0:T(8,128)S(1)}, f32[8,64,64]{2,1,0:T(8,128)}, u32[]{:S(2)}) %copy-start) | copy-done | bytes 131096
  4.0 0.0 copy-start.1
  4.0 0.9 %copy-done.1 = f32[8,64,64]{2,1,0:T(8,128)S(1)} copy-done((f32[8,64,64]{2,1,0:T(8,128)S(1)}, f32[8,64,64]{2,1,0:T(8,128)}, u32[]{:S(2)}) %copy-start.1) | copy-done | bytes 131096
  4.9 0.0 copy-start.2
  4.9 0.9 %copy-done.2 = f32[8,64,64]{2,1,0:T(8,128)S(1)} copy-done((f32[8,64,64]{2,1,0:T(8,128)S(1)}, f32[8,64,64]{2,1,0:T(8,128)}, u32[]{:S(2)}) %copy-start.2) | copy-done | bytes 131096
  5.9 0.0 copy-start.3
  5.9 0.9 %copy-done.3 = f32[32,32,3,3]{1,0,3,2:T(8,128)S(1)} copy-done((f32[32,32,3,3]{1,0,3,2:T(8,128)S(1)}, f32[32,32,3,3]{1,0,3,2:T(8,128)}, u32[]{:S(2)}) %copy-start.3) | copy-done | bytes 36888
  6.8 0.0 copy-start.4
  6.8 0.9 %copy-done.4 = f32[32,32,3,3]{1,0,3,2:T(8,128)S(1)} copy-done((f32[32,32,3,3]{1,0,3,2:T(8,128)S(1)}, f32[32,32,3,3]{1,0,3,2:T(8,128)}, u32[]{:S(2)}) %copy-start.4) | copy-done | bytes 36888
  7.7 0.0 copy-start.5
  7.7 0.7 %copy-done.5 = s32[8,1]{0,1:T(1,128)S(1)} copy-done((s32[8,1]{0,1:T(1,128)S(1)}, s32[8,1]{0,1:T(1,128)}, u32[]{:S(2)}) %copy-start.5) | copy-done | bytes 56
  8.3 0.0 copy-start.6
  8.3 0.7 %copy-done.6 = s32[8]{0:T(128)S(1)} copy-done((s32[8]{0:T(128)S(1)}, s32[8]{0:T(128)}, u32[]{:S(2)}) %copy-start.6) | copy-done | bytes 56
  9.0 0.0 copy-start.7
  9.0 0.7 %copy-done.7 = s32[8]{0:T(128)S(1)} copy-done((s32[8]{0:T(128)S(1)}, s32[8]{0:T(128)}, u32[]{:S(2)}) %copy-start.7) | copy-done | bytes 56
  9.6 0.7 %copy-done.8 = f32[8]{0:T(128)S(1)} copy-done((f32[8]{0:T(128)S(1)}, f32[8]{0:T(128)}, u32[]{:S(2)}) %copy-start.8) | copy-done | bytes 56
  10.3 21.7 %coadd.1 = (f32[152,256]{1,0:T(8,128)S(1)}, bf16[256,256]{1,0:T(8,128)(2,1)S(1)}, bf16[2,3,192,256]{3,2,1,0:T(8,128)(2,1)S(1)}, bf16[2,3,192,256]{3,2,1,0:T(8,128)(2,1)S(1)}) custom-call(s32[8]{0:T(128)S(1)} %bitcast.13, s32[8]{0:T(128)S(1)} %copy-done.6, s32[8]{0:T(128)S(1)} %copy-done.7, f32[8]{0:T(128)S(1)} %copy-done.8, f32[8,64,64]{2,1,0:T(8,128)S(1)} %copy-done, ...), custom_call_target="tpu_custom_call" | custom-call | tf_op jit(solution)/shard_map/coadd/pallas_call | solution.py:318
  32.0 26.6 %convs.1 = f32[4096,128]{1,0:T(8,128)} custom-call(f32[152,256]{1,0:T(8,128)S(1)} %get-tuple-element.9.refs_0_, bf16[256,256]{1,0:T(8,128)(2,1)S(1)} %get-tuple-element.10.refs_1_, bf16[2,3,192,256]{3,2,1,0:T(8,128)(2,1)S(1)} %get-tuple-element.11.refs_2_, bf16[2,3,192,256]{3,2,1,0:T(8,128)(2,1)S(1)} %get-tuple-element.12.refs_3_, ...), custom_call_target="tpu_custom_call" | custom-call | tf_op jit(solution)/shard_map/convs/pallas_call | solution.py:144
  (2 shorter events, 0.0 us)
Async XLA Ops:
  3.0 1.0 %copy-start = (f32[8,64,64]{2,1,0:T(8,128)S(1)}, f32[8,64,64]{2,1,0:T(8,128)}, u32[]{:S(2)}) copy-start(f32[8,64,64]{2,1,0:T(8,128)} %tiles.1) | copy-start | bytes 393220
  4.0 0.9 %copy-start.1 = (f32[8,64,64]{2,1,0:T(8,128)S(1)}, f32[8,64,64]{2,1,0:T(8,128)}, u32[]{:S(2)}) copy-start(f32[8,64,64]{2,1,0:T(8,128)} %rker.1) | copy-start | bytes 393220
  4.9 0.9 %copy-start.2 = (f32[8,64,64]{2,1,0:T(8,128)S(1)}, f32[8,64,64]{2,1,0:T(8,128)}, u32[]{:S(2)}) copy-start(f32[8,64,64]{2,1,0:T(8,128)} %cker.1) | copy-start | bytes 393220
  5.9 0.9 %copy-start.3 = (f32[32,32,3,3]{1,0,3,2:T(8,128)S(1)}, f32[32,32,3,3]{1,0,3,2:T(8,128)}, u32[]{:S(2)}) copy-start(f32[32,32,3,3]{1,0,3,2:T(8,128)} %param.22) | copy-start | bytes 110596
  6.8 0.9 %copy-start.4 = (f32[32,32,3,3]{1,0,3,2:T(8,128)S(1)}, f32[32,32,3,3]{1,0,3,2:T(8,128)}, u32[]{:S(2)}) copy-start(f32[32,32,3,3]{1,0,3,2:T(8,128)} %param.24) | copy-start | bytes 110596
  7.7 0.7 %copy-start.5 = (s32[8,1]{0,1:T(1,128)S(1)}, s32[8,1]{0,1:T(1,128)}, u32[]{:S(2)}) copy-start(s32[8,1]{0,1:T(1,128)} %param.16) | copy-start | bytes 100
  8.3 0.7 %copy-start.6 = (s32[8]{0:T(128)S(1)}, s32[8]{0:T(128)}, u32[]{:S(2)}) copy-start(s32[8]{0:T(128)} %roff.1) | copy-start | bytes 100
  9.0 0.7 %copy-start.7 = (s32[8]{0:T(128)S(1)}, s32[8]{0:T(128)}, u32[]{:S(2)}) copy-start(s32[8]{0:T(128)} %coff.1) | copy-start | bytes 100
  9.6 0.7 %copy-start.8 = (f32[8]{0:T(128)S(1)}, f32[8]{0:T(128)}, u32[]{:S(2)}) copy-start(f32[8]{0:T(128)} %wgt.1) | copy-start | bytes 100

commit v2 on v1

--- a/solution.py
+++ b/solution.py
@@ -15,7 +15,7 @@
     return hi, (x - hi.astype(F32)).astype(BF)
 
 
-def build_weights(f1_ref, b1_ref, f2_ref, f3_ref, w1_ref, w2_ref, w3_ref):
+def build_weights(f1_ref, vec_ref, f2_ref, f3_ref, w1_ref, w2_ref, w3_ref, bias_ref):
     for f_ref, w_ref in ((f2_ref, w2_ref), (f3_ref, w3_ref)):
         for dx in range(3):
             row = jnp.concatenate(
@@ -25,24 +25,29 @@
                 hi, lo = split(moved)
                 w_ref[0, dx, yo * 32:(yo + 1) * 32, :] = hi
                 w_ref[1, dx, yo * 32:(yo + 1) * 32, :] = lo
-    f1 = f1_ref[...]
-    hi, lo = split(f1)
+    rows = jnp.concatenate([f1_ref[k] for k in range(9)] + [vec_ref[k] for k in range(3)]
+                           + [jnp.zeros((116, 32), F32)], axis=0)
+    rows = jnp.concatenate([rows, jnp.zeros((128, 96), F32)], axis=1)
+    turned = jnp.transpose(rows)[:32, :]
+    hi, lo = split(turned)
     hi = hi.astype(F32)
     lo = lo.astype(F32)
-    b = b1_ref[...]
-    bhi, blo = split(b)
     lane = lax.broadcasted_iota(jnp.int32, (32, 256), 1)
+    base = jnp.where(lane == 144, hi[:, 9:10], 0.0) + jnp.where(lane == 145, lo[:, 9:10], 0.0)
     for yo in range(8):
-        acc = jnp.where(lane == 144, bhi.astype(F32), 0.0) + jnp.where(lane == 145, blo.astype(F32), 0.0)
+        acc = base
         for part, w in enumerate((hi, hi, lo)):
             for dx in range(3):
                 for dy in range(3):
-                    acc = acc + jnp.where(lane == part * 48 + dx * 16 + yo + dy, w[:, dy * 3 + dx:dy * 3 + dx + 1], 0.0)
+                    k = dy * 3 + dx
+                    acc = jnp.where(lane == part * 48 + dx * 16 + yo + dy, w[:, k:k + 1], acc)
         r = (yo % 2) * 128 + (yo // 2) * 32
         w1_ref[r:r + 32, :] = acc.astype(BF)
-
-
-def conv_body(row, col, p_ref, w1_ref, w2_ref, w3_ref, b2_ref, b3_ref, out_ref,
+    for k in range(2):
+        bias_ref[k] = jnp.broadcast_to(turned[:, 10 + k:11 + k], (32, 128))
+
+
+def conv_body(row, col, p_ref, w1_ref, w2_ref, w3_ref, bias_ref, out_ref,
               ps, f_hi, f_lo, s_hi, s_lo):
     p = p_ref[...]
     ps[0] = pltpu.roll(p, 1, 1)
@@ -63,7 +68,7 @@
         yy = base + y
         return jnp.where(jnp.logical_and(yy >= 0, yy < n_rows), 1.0, 0.0)
 
-    @pl.loop(0, 18)
+    @pl.loop(0, 18, unroll=3)
     def _(g):
         hs, ls = [], []
         for dx in range(3):
@@ -81,9 +86,9 @@
                 f_hi[q, at, :] = h
                 f_lo[q, at, :] = l
 
-    b2 = b2_ref[...]
-
-    @pl.loop(0, 24)
+    b2 = jnp.concatenate([bias_ref[0], bias_ref[0]], axis=1)
+
+    @pl.loop(0, 24, unroll=4)
     def _(t):
         q = lax.rem(t, 2)
         m0 = jnp.minimum(6 * (t // 2), 62)
@@ -108,21 +113,21 @@
                 s_hi[k, r, at, :] = h
                 s_lo[k, r, at, :] = l
 
-    b3 = b3_ref[...][:, :128]
-
-    @pl.loop(0, 12)
+    b3 = bias_ref[1]
+
+    @pl.loop(0, 12, unroll=4)
     def _(t):
         half = lax.rem(t, 2)
         n0 = jnp.minimum(6 * (t // 2), 26)
         at = pl.ds(pl.multiple_of(32 * n0, 64), 256)
-        acc = None
+        hs, ls, wh, wl = [], [], [], []
         for dx in range(3):
-            hi = jnp.concatenate([s_hi[dx, 2 * half, at, :], s_hi[dx, 2 * half + 1, at, :]], axis=1)
-            lo = jnp.concatenate([s_lo[dx, 2 * half, at, :], s_lo[dx, 2 * half + 1, at, :]], axis=1)
-            part = (jnp.dot(w3_ref[0, dx], hi, preferred_element_type=F32)
-                    + jnp.dot(w3_ref[1, dx], hi, preferred_element_type=F32)
-                    + jnp.dot(w3_ref[0, dx], lo, preferred_element_type=F32))
-            acc = part if acc is None else acc + part
+            hs.append(jnp.concatenate([s_hi[dx, 2 * half, at, :], s_hi[dx, 2 * half + 1, at, :]], axis=1))
+            ls.append(jnp.concatenate([s_lo[dx, 2 * half, at, :], s_lo[dx, 2 * half + 1, at, :]], axis=1))
+            wh.append(w3_ref[0, dx])
+            wl.append(w3_ref[1, dx])
+        acc = jnp.dot(jnp.concatenate(wh + wl + wh, axis=1), jnp.concatenate(hs + hs + ls, axis=0),
+                      preferred_element_type=F32)
         for e in range(2):
             for yo in range(6):
                 v = acc[yo * 32:yo * 32 + 32, e * 128:e * 128 + 128] + b3
@@ -136,22 +141,22 @@
 
 
 W_SHAPES = [jax.ShapeDtypeStruct((256, 256), BF), jax.ShapeDtypeStruct((2, 3, 192, 256), BF),
-            jax.ShapeDtypeStruct((2, 3, 192, 256), BF)]
-
-
-def conv_call(p, w1, w2, w3, b2, b3):
+            jax.ShapeDtypeStruct((2, 3, 192, 256), BF), jax.ShapeDtypeStruct((2, 32, 128), F32)]
+
+
+def conv_call(p, w1, w2, w3, bias):
     vm = pl.BlockSpec(memory_space=pltpu.VMEM)
     return pl.pallas_call(
         conv_kernel,
         out_shape=jax.ShapeDtypeStruct((4096, 128), F32),
-        in_specs=[vm] * 6,
+        in_specs=[vm] * 5,
         out_specs=vm,
         scratch_shapes=[pltpu.VMEM((3, 152, 256), F32),
                         pltpu.VMEM((2, 74 * 32, 256), BF), pltpu.VMEM((2, 74 * 32, 256), BF),
                         pltpu.VMEM((3, 4, 34 * 32, 128), BF), pltpu.VMEM((3, 4, 34 * 32, 128), BF)],
         compiler_params=pltpu.CompilerParams(vmem_limit_bytes=48 << 20),
         name="convs",
-    )(p, w1, w2, w3, b2, b3)
+    )(p, w1, w2, w3, bias)
 
 
 N_ROW = 8
@@ -166,10 +171,16 @@
     return d(ah, bh) + d(al, bh) + d(ah, bl)
 
 
-def comm_kernel(dest, roff, coff, wgt, tiles, rker, cker, f1_ref, b1_ref, f2_ref, f3_ref,
-                p_ref, w1_ref, w2_ref, w3_ref,
-                ckpad, packed, send, recv, spread, edge_out, edge_in,
-                send_sem, recv_sem, esend_sem, erecv_sem):
+def comm_kernel(dest_h, roff_h, coff_h, wgt_h, tiles_h, rker_h, cker_h, f1_h, b1_h, f2_h, b2_h, f3_h, b3_h,
+                p_ref, w1_ref, w2_ref, w3_ref, bias_ref,
+                dest, roff, coff, wgt, tiles, rker, ckpad, f1, vec, f2, f3, packed, send, recv, spread, pick,
+                edge_out, edge_in, in_sem, send_sem, recv_sem, esend_sem, erecv_sem):
+    fetches = [pltpu.make_async_copy(src, dst, in_sem.at[i]) for i, (src, dst) in enumerate((
+        (rker_h, rker), (tiles_h, tiles), (cker_h, ckpad.at[:, pl.ds(TS, TS), :]), (coff_h, coff),
+        (dest_h, dest), (roff_h, roff), (wgt_h, wgt), (f2_h, f2), (f3_h, f3),
+        (f1_h, f1), (b1_h, vec.at[0]), (b2_h, vec.at[1]), (b3_h, vec.at[2])))]
+    for f in fetches:
+        f.start()
     row = lax.axis_index("row")
     col = lax.axis_index("col")
     up = lax.rem(row + N_ROW - 1, N_ROW)
@@ -187,33 +198,36 @@
         for c in (left, col, right):
             pl.semaphore_signal(barrier, inc=1, device_id=(r, c), device_id_type=MESH)
 
-    ckpad[...] = jnp.zeros_like(ckpad)
-
-    @pl.loop(0, TILES_DEV)
-    def _(t):
+    blank = jnp.zeros((TILES_DEV, TS, TS), F32)
+    ckpad[:, 0:TS, :] = blank
+    ckpad[:, 2 * TS:3 * TS, :] = blank
+    for f in fetches[:4]:
+        f.wait()
+    for t in range(TILES_DEV):
         rh, rl = split(rker[t])
         th, tl = split(tiles[t])
         mid = dot3(rh, rl, th, tl, ((1,), (0,)))
-        ckpad[TS:2 * TS, :] = cker[t]
-        placed = ckpad[pl.ds(TS - coff[t], 2 * TS), :]
+        placed = ckpad[t, pl.ds(TS - coff[0, t], 2 * TS), :]
         mh, ml = split(mid)
         ch, cl = split(placed)
         img = dot3(mh, ml, ch, cl, ((1,), (1,)))
         packed[t] = img[:32, :] + pltpu.roll(img[32:, :], 64, 1)
+    for f in fetches[4:7]:
+        f.wait()
 
     sub8 = lax.broadcasted_iota(jnp.int32, (8, 128), 0)
 
-    @pl.loop(0, N_COL)
+    @pl.loop(0, N_COL, unroll=4)
     def _(c):
         acc = None
         ro = jnp.float32(0.0)
         co = jnp.float32(0.0)
         w = jnp.float32(0.0)
         for t in range(TILES_DEV):
-            hit = jnp.where(dest[t] == c, 1.0, 0.0)
-            wt = hit * wgt[t]
-            ro = ro + hit * roff[t].astype(F32)
-            co = co + hit * coff[t].astype(F32)
+            hit = jnp.where(dest[0, t] == c, 1.0, 0.0)
+            wt = hit * wgt[0, t]
+            ro = ro + hit * roff[0, t].astype(F32)
+            co = co + hit * coff[0, t].astype(F32)
             w = w + wt
             term = packed[t] * wt
             acc = term if acc is None else acc + term
@@ -233,22 +247,21 @@
         tile_copy(k).start()
 
     recv[0] = send[col]
-    build_weights(f1_ref, b1_ref, f2_ref, f3_ref, w1_ref, w2_ref, w3_ref)
-
-    @pl.loop(1, N_COL)
-    def _(k):
-        tile_copy(k).wait()
+    for f in fetches[7:]:
+        f.wait()
+    build_weights(f1, vec, f2, f3, w1_ref, w2_ref, w3_ref, bias_ref)
 
     lane = lax.broadcasted_iota(jnp.int32, (1, 128), 1).astype(F32)
     suby = lax.broadcasted_iota(jnp.int32, (128, 128), 0).astype(F32)
     lanes = lax.broadcasted_iota(jnp.int32, (128, 128), 1)
     lane_a = (lanes % TS).astype(F32)
     cover = jnp.zeros((128, 128), F32)
-    numer = jnp.zeros((128, 256), F32)
     for pair in range(N_COL // 2):
         ros = []
         for e in range(2):
             s = 2 * pair + e
+            if s > 0:
+                tile_copy(s).wait()
             pk = recv[s, 0:32, :]
             ro = recv[s, 32:33, :]
             co = recv[s, 33:34, :]
@@ -267,8 +280,8 @@
             cover = cover + jnp.where(jnp.logical_and(dy >= 0.0, dy < float(TS)), wcol, 0.0)
             ros.append(ro)
         want = jnp.where(lanes < TS, ros[0], ros[1]) + lane_a
-        pick = jnp.where(suby == want, 1.0, 0.0).astype(BF)
-        numer = numer + jnp.dot(pick, spread[pair * 128:pair * 128 + 128, :], preferred_element_type=F32)
+        pick[:, pair * 128:pair * 128 + 128] = jnp.where(suby == want, 1.0, 0.0).astype(BF)
+    numer = jnp.dot(pick[...], spread[...], preferred_element_type=F32)
     coadd = (numer[:, :128] + numer[:, 128:]) / (1.0 + cover)
 
     edge_out[0] = coadd[0:8, :]
@@ -312,22 +325,34 @@
         p_ref[7 + 8 * k:15 + 8 * k, 128:256] = jnp.where(lane8 < TS, r, l) * side
 
 
-def comm_call(dest, roff, coff, wgt, tiles, rker, cker, f1, b1, f2, f3):
+def comm_call(*args):
     vm = pl.BlockSpec(memory_space=pltpu.VMEM)
-    sm = pl.BlockSpec(memory_space=pltpu.SMEM)
+    hbm = pl.BlockSpec(memory_space=pltpu.HBM)
     return pl.pallas_call(
         comm_kernel,
         out_shape=[jax.ShapeDtypeStruct((152, 256), F32)] + W_SHAPES,
-        in_specs=[sm] * 4 + [vm] * 7,
-        out_specs=[vm] * 4,
+        in_specs=[hbm] * 13,
+        out_specs=[vm] * 5,
         scratch_shapes=[
-            pltpu.VMEM((3 * TS, TS), F32),
+            pltpu.SMEM((1, TILES_DEV), jnp.int32),
+            pltpu.SMEM((1, TILES_DEV), jnp.int32),
+            pltpu.SMEM((1, TILES_DEV), jnp.int32),
+            pltpu.SMEM((1, TILES_DEV), F32),
+            pltpu.VMEM((TILES_DEV, TS, TS), F32),
+            pltpu.VMEM((TILES_DEV, TS, TS), F32),
+            pltpu.VMEM((TILES_DEV, 3 * TS, TS), F32),
+            pltpu.VMEM((9, 1, 32), F32),
+            pltpu.VMEM((3, 1, 32), F32),
+            pltpu.VMEM((9, 32, 32), F32),
+            pltpu.VMEM((9, 32, 32), F32),
             pltpu.VMEM((TILES_DEV, 32, 128), F32),
             pltpu.VMEM((N_COL, 40, 128), F32),
             pltpu.VMEM((N_COL, 40, 128), F32),
             pltpu.VMEM((N_COL * TS, 256), BF),
+            pltpu.VMEM((128, N_COL * TS), BF),
             pltpu.VMEM((4, 8, 128), F32),
             pltpu.VMEM((8, 8, 128), F32),
+            pltpu.SemaphoreType.DMA((13,)),
             pltpu.SemaphoreType.DMA((N_COL,)),
             pltpu.SemaphoreType.DMA((N_COL,)),
             pltpu.SemaphoreType.DMA((8,)),
@@ -335,18 +360,20 @@
         ],
         compiler_params=pltpu.CompilerParams(collective_id=0, has_side_effects=True, vmem_limit_bytes=32 << 20),
         name="coadd",
-    )(dest, roff, coff, wgt, tiles, rker, cker, f1, b1, f2, f3)
+    )(*args)
 
 
 def body(tiles, row_kernels, column_resample_kernels, destination, row_offset, col_offset, exposure_weight,
          first_filter, first_bias, second_filter, second_bias, third_filter, third_bias):
+    line = lambda v: v.reshape(1, -1)
     taps = lambda f: jnp.transpose(f, (2, 3, 0, 1)).reshape(9, 32, 32)
-    wide = lambda b: jnp.broadcast_to(b[:, None], (32, 256))
-    p, w1, w2, w3 = comm_call(destination[:, 0], row_offset, col_offset, exposure_weight, tiles, row_kernels,
-                              column_resample_kernels, first_filter.reshape(32, 9), first_bias[:, None],
-                              taps(second_filter), taps(third_filter))
-    out = conv_call(p, w1, w2, w3, wide(second_bias), wide(third_bias))
-    return out.reshape(32, 128, 128)
+    one = jnp.transpose(first_filter, (2, 3, 1, 0)).reshape(9, 1, 32)
+    keep = lambda v: pltpu.with_memory_space_constraint(v, pltpu.HBM)
+    p, w1, w2, w3, bias = comm_call(*map(keep, (
+        destination.T, line(row_offset), line(col_offset), line(exposure_weight), tiles, row_kernels,
+        column_resample_kernels, one, line(first_bias), taps(second_filter), line(second_bias),
+        taps(third_filter), line(third_bias))))
+    return conv_call(p, w1, w2, w3, bias).reshape(32, 128, 128)
 
 
 def solution(mesh):

time: 58.9 us -> 38 us (0.65)
  Pallas kernels: 48.3 us -> 37.8 us
  local copies, waits for them, and re-layouts: 9.57 us -> 0 us
  other arithmetic: 0.71 us -> 0 us
    pallas_call x1, Pallas kernels: 26.6 us -> 16.8 us  [conv_call(): pl.pallas_call(conv_kernel, out_shape=jax.ShapeDtypeStruct((4096, 128), F...]
    unnamed x18 -> x0, local copies, waits for them, and re-layouts: 7.29 us -> none
    broadcast_in_dim x3 -> x0, local copies, waits for them, and re-layouts: 2.19 us -> none  [the longest x2 1.45 us: body(): wide = lambda b: jnp.broadcast_to(b[:, None], (32, 256))]
    unnamed x1 -> x0, other arithmetic: 0.71 us -> none
where the time goes in v2:
time: 38 us; the launch traced here: 37.9 us
  Pallas kernels  37.8 us (99%)
    pallas_call x1, Pallas kernels, comm_call(): pl.pallas_call(comm_kernel, out_shape=[jax.ShapeDtypeStruct((152, 256), F...  21.1 us
    pallas_call x1, Pallas kernels, conv_call(): pl.pallas_call(conv_kernel, out_shape=jax.ShapeDtypeStruct((4096, 128), F...  16.8 us

profile of v2, /device:TPU:1, one launch (start us, length us, event | category | flops | bytes accessed | tf_op | source)
XLA Modules:
  0.0 37.9 jit_solution(7100368628115482601)
XLA Ops:
  0.0 21.1 %coadd.1 = (f32[152,256]{1,0:T(8,128)S(1)}, bf16[256,256]{1,0:T(8,128)(2,1)S(1)}, bf16[2,3,192,256]{3,2,1,0:T(8,128)(2,1)S(1)}, bf16[2,3,192,256]{3,2,1,0:T(8,128)(2,1)S(1)}, f32[2,32,128]{2,1,0:T(8,128)S(1)}) custom-call(s32[1,8]{1,0:T(1,128)} %bitcast.20, s32[1,8]{1,0:T(1,128)} %bitcast.21, s32[1,8]{1,0:T(1,128)} %bitcast.22, f32[1,8]{1,0:T(1,128)} %bitcast.23, ...), custom_call_target="tpu_custom_call" | custom-call | tf_op jit(solution)/shard_map/coadd/pallas_call | solution.py:331
  21.1 16.8 %convs.1 = f32[4096,128]{1,0:T(8,128)} custom-call(f32[152,256]{1,0:T(8,128)S(1)} %get-tuple-element.10.refs_0_, bf16[256,256]{1,0:T(8,128)(2,1)S(1)} %get-tuple-element.11.refs_1_, bf16[2,3,192,256]{3,2,1,0:T(8,128)(2,1)S(1)} %get-tuple-element.12.refs_2_, bf16[2,3,192,256]{3,2,1,0:T(8,128)(2,1)S(1)} %get-tuple-element.13.refs_3_, ...), custom_call_target="tpu_custom_call" | custom-call | tf_op jit(solution)/shard_map/convs/pallas_call | solution.py:149

commit v3 on v2

--- a/solution.py
+++ b/solution.py
@@ -48,7 +48,7 @@
 
 
 def conv_body(row, col, p_ref, w1_ref, w2_ref, w3_ref, bias_ref, out_ref,
-              ps, f_hi, f_lo, s_hi, s_lo):
+              ps, f_hi, f_lo, s_hi, s_lo, out_s, out_sem):
     p = p_ref[...]
     ps[0] = pltpu.roll(p, 1, 1)
     ps[1] = p
@@ -68,7 +68,7 @@
         yy = base + y
         return jnp.where(jnp.logical_and(yy >= 0, yy < n_rows), 1.0, 0.0)
 
-    @pl.loop(0, 18, unroll=3)
+    @pl.loop(0, 18, unroll=6)
     def _(g):
         hs, ls = [], []
         for dx in range(3):
@@ -88,7 +88,7 @@
 
     b2 = jnp.concatenate([bias_ref[0], bias_ref[0]], axis=1)
 
-    @pl.loop(0, 24, unroll=4)
+    @pl.loop(0, 24, unroll=12)
     def _(t):
         q = lax.rem(t, 2)
         m0 = jnp.minimum(6 * (t // 2), 62)
@@ -115,25 +115,31 @@
 
     b3 = bias_ref[1]
 
-    @pl.loop(0, 12, unroll=4)
-    def _(t):
-        half = lax.rem(t, 2)
-        n0 = jnp.minimum(6 * (t // 2), 26)
-        at = pl.ds(pl.multiple_of(32 * n0, 64), 256)
-        hs, ls, wh, wl = [], [], [], []
-        for dx in range(3):
-            hs.append(jnp.concatenate([s_hi[dx, 2 * half, at, :], s_hi[dx, 2 * half + 1, at, :]], axis=1))
-            ls.append(jnp.concatenate([s_lo[dx, 2 * half, at, :], s_lo[dx, 2 * half + 1, at, :]], axis=1))
-            wh.append(w3_ref[0, dx])
-            wl.append(w3_ref[1, dx])
-        acc = jnp.dot(jnp.concatenate(wh + wl + wh, axis=1), jnp.concatenate(hs + hs + ls, axis=0),
-                      preferred_element_type=F32)
-        for e in range(2):
-            for yo in range(6):
-                v = acc[yo * 32:yo * 32 + 32, e * 128:e * 128 + 128] + b3
-                y = 4 * (n0 + yo) + 2 * half + e
-                for k in range(4):
-                    out_ref[pl.ds(k * 1024 + y, 8, stride=128), :] = v[8 * k:8 * k + 8, :]
+    whole = out_s.reshape(32, 128, 128)
+    writes = []
+    for step, (n0, first, count) in enumerate(
+            ((0, 0, 24), (6, 24, 24), (12, 48, 24), (18, 72, 24), (24, 96, 8), (26, 104, 24))):
+        at = pl.ds(32 * n0, 256)
+        for half in range(2):
+            hs, ls, wh, wl = [], [], [], []
+            for dx in range(3):
+                hs.append(jnp.concatenate([s_hi[dx, 2 * half, at, :], s_hi[dx, 2 * half + 1, at, :]], axis=1))
+                ls.append(jnp.concatenate([s_lo[dx, 2 * half, at, :], s_lo[dx, 2 * half + 1, at, :]], axis=1))
+                wh.append(w3_ref[0, dx])
+                wl.append(w3_ref[1, dx])
+            acc = jnp.dot(jnp.concatenate(wh + wl + wh, axis=1), jnp.concatenate(hs + hs + ls, axis=0),
+                          preferred_element_type=F32)
+            for e in range(2):
+                for yo in range(6):
+                    v = acc[yo * 32:yo * 32 + 32, e * 128:e * 128 + 128] + b3
+                    y = 4 * (n0 + yo) + 2 * half + e
+                    for k in range(4):
+                        out_s[pl.ds(k * 1024 + y, 8, stride=128), :] = v[8 * k:8 * k + 8, :]
+        rows = pl.ds(first, count)
+        writes.append(pltpu.make_async_copy(whole.at[:, rows, :], out_ref.at[:, rows, :], out_sem.at[step]))
+        writes[-1].start()
+    for w in writes:
+        w.wait()
 
 
 def conv_kernel(*refs):
@@ -148,12 +154,13 @@
     vm = pl.BlockSpec(memory_space=pltpu.VMEM)
     return pl.pallas_call(
         conv_kernel,
-        out_shape=jax.ShapeDtypeStruct((4096, 128), F32),
+        out_shape=jax.ShapeDtypeStruct((32, 128, 128), F32),
         in_specs=[vm] * 5,
-        out_specs=vm,
+        out_specs=pl.BlockSpec(memory_space=pltpu.HBM),
         scratch_shapes=[pltpu.VMEM((3, 152, 256), F32),
                         pltpu.VMEM((2, 74 * 32, 256), BF), pltpu.VMEM((2, 74 * 32, 256), BF),
-                        pltpu.VMEM((3, 4, 34 * 32, 128), BF), pltpu.VMEM((3, 4, 34 * 32, 128), BF)],
+                        pltpu.VMEM((3, 4, 34 * 32, 128), BF), pltpu.VMEM((3, 4, 34 * 32, 128), BF),
+                        pltpu.VMEM((4096, 128), F32), pltpu.SemaphoreType.DMA((6,))],
         compiler_params=pltpu.CompilerParams(vmem_limit_bytes=48 << 20),
         name="convs",
     )(p, w1, w2, w3, bias)
@@ -164,6 +171,7 @@
 TILES_DEV = 8
 TS = 64
 MESH = pl.DeviceIdType.MESH
+ORDER = (10, 1, 4, 3, 12, 2, 8, 5, 15, 7, 13, 6, 9, 14, 11)
 
 
 def dot3(ah, al, bh, bl, dims):
@@ -242,8 +250,7 @@
             src_ref=send.at[c], dst_ref=recv.at[k], send_sem=send_sem.at[k], recv_sem=recv_sem.at[k],
             device_id=(row, c), device_id_type=MESH)
 
-    @pl.loop(1, N_COL)
-    def _(k):
+    for k in ORDER:
         tile_copy(k).start()
 
     recv[0] = send[col]
@@ -261,13 +268,14 @@
         for e in range(2):
             s = 2 * pair + e
             if s > 0:
-                tile_copy(s).wait()
-            pk = recv[s, 0:32, :]
-            ro = recv[s, 32:33, :]
-            co = recv[s, 33:34, :]
-            w = recv[s, 34:35, :]
-            at = lane - co
-            inside = jnp.logical_and(at >= 0.0, at < float(TS))
+                tile_copy(ORDER[s - 1]).wait()
+            at = ORDER[s - 1] if s > 0 else 0
+            pk = recv[at, 0:32, :]
+            ro = recv[at, 32:33, :]
+            co = recv[at, 33:34, :]
+            w = recv[at, 34:35, :]
+            off = lane - co
+            inside = jnp.logical_and(off >= 0.0, off < float(TS))
             a = jnp.where(inside, pk, 0.0)
             b = jnp.where(inside, pltpu.roll(pk, 64, 1), 0.0)
             for half, v in enumerate((a, b)):
@@ -373,7 +381,7 @@
         destination.T, line(row_offset), line(col_offset), line(exposure_weight), tiles, row_kernels,
         column_resample_kernels, one, line(first_bias), taps(second_filter), line(second_bias),
         taps(third_filter), line(third_bias))))
-    return conv_call(p, w1, w2, w3, bias).reshape(32, 128, 128)
+    return conv_call(p, w1, w2, w3, bias)
 
 
 def solution(mesh):

time: 38 us -> 34.5 us (0.908)
  Pallas kernels: 37.8 us -> 34.3 us
    pallas_call x1, Pallas kernels: 16.8 us -> 13.6 us  [conv_call(): pl.pallas_call(conv_kernel, out_shape=jax.ShapeDtypeStruct((32, 128, 128)...]
    pallas_call x1, Pallas kernels: 21.1 us -> 20.7 us  [comm_call(): pl.pallas_call(comm_kernel, out_shape=[jax.ShapeDtypeStruct((152, 256), F...]
where the time goes in v3:
time: 34.5 us; the launch traced here: 34.3 us
  Pallas kernels  34.3 us (99%)
    pallas_call x1, Pallas kernels, comm_call(): pl.pallas_call(comm_kernel, out_shape=[jax.ShapeDtypeStruct((152, 256), F...  20.7 us
    pallas_call x1, Pallas kernels, conv_call(): pl.pallas_call(conv_kernel, out_shape=jax.ShapeDtypeStruct((32, 128, 128)...  13.6 us

profile of v3, /device:TPU:1, one launch (start us, length us, event | category | flops | bytes accessed | tf_op | source)
XLA Modules:
  0.0 34.3 jit_solution(6249899054995653588)
XLA Ops:
  0.0 20.7 %coadd.1 = (f32[152,256]{1,0:T(8,128)S(1)}, bf16[256,256]{1,0:T(8,128)(2,1)S(1)}, bf16[2,3,192,256]{3,2,1,0:T(8,128)(2,1)S(1)}, bf16[2,3,192,256]{3,2,1,0:T(8,128)(2,1)S(1)}, f32[2,32,128]{2,1,0:T(8,128)S(1)}) custom-call(s32[1,8]{1,0:T(1,128)} %bitcast.19, s32[1,8]{1,0:T(1,128)} %bitcast.20, s32[1,8]{1,0:T(1,128)} %bitcast.21, f32[1,8]{1,0:T(1,128)} %bitcast.22, ...), custom_call_target="tpu_custom_call" | custom-call | tf_op jit(solution)/shard_map/coadd/pallas_call | solution.py:339
  20.7 13.6 %convs.1 = f32[32,128,128]{2,1,0:T(8,128)} custom-call(f32[152,256]{1,0:T(8,128)S(1)} %get-tuple-element.10.refs_0_, bf16[256,256]{1,0:T(8,128)(2,1)S(1)} %get-tuple-element.11.refs_1_, bf16[2,3,192,256]{3,2,1,0:T(8,128)(2,1)S(1)} %get-tuple-element.12.refs_2_, bf16[2,3,192,256]{3,2,1,0:T(8,128)(2,1)S(1)} %get-tuple-element.13.refs_3_, ...), custom_call_target="tpu_custom_call" | custom-call | tf_op jit(solution)/shard_map/convs/pallas_call | solution.py:155

commit v4 on v3

--- a/solution.py
+++ b/solution.py
@@ -68,7 +68,7 @@
         yy = base + y
         return jnp.where(jnp.logical_and(yy >= 0, yy < n_rows), 1.0, 0.0)
 
-    @pl.loop(0, 18, unroll=6)
+    @pl.loop(0, 18, unroll=18)
     def _(g):
         hs, ls = [], []
         for dx in range(3):
@@ -88,53 +88,68 @@
 
     b2 = jnp.concatenate([bias_ref[0], bias_ref[0]], axis=1)
 
-    @pl.loop(0, 24, unroll=12)
-    def _(t):
-        q = lax.rem(t, 2)
-        m0 = jnp.minimum(6 * (t // 2), 62)
-        at = pl.ds(pl.multiple_of(32 * m0, 64), 256)
-        hi = f_hi[q, at, :]
-        lo = f_lo[q, at, :]
+    def second(hi, lo, places):
         parts = []
         for dx in range(3):
             parts.append(jnp.dot(w2_ref[0, dx], hi, preferred_element_type=F32)
                          + jnp.dot(w2_ref[1, dx], hi, preferred_element_type=F32)
                          + jnp.dot(w2_ref[0, dx], lo, preferred_element_type=F32))
         acc = parts[1] + pltpu.roll(parts[0], 2, 1) + pltpu.roll(parts[2], 254, 1)
-        n0 = m0 // 2
-        for yo in range(6):
-            mask = cmask * valid(2 * (m0 + yo) + q - 4)
-            v = acc[yo * 32:yo * 32 + 32, :]
-            v = jnp.maximum(v + b2, 0.0) * mask
-            r = 2 * (yo % 2) + q
-            at = pl.ds(pl.multiple_of((n0 + yo // 2) * 32, 32), 32)
+        for yo, y, r, n in places:
+            mask = cmask * valid(y)
+            v = jnp.maximum(acc[yo * 32:yo * 32 + 32, :] + b2, 0.0) * mask
+            at = pl.ds(pl.multiple_of(n * 32, 32), 32)
             for k, sh in enumerate((pltpu.roll(v, 4, 1), v, pltpu.roll(v, 252, 1))):
                 h, l = split(sh[:, :128])
                 s_hi[k, r, at, :] = h
                 s_lo[k, r, at, :] = l
 
+    @pl.loop(0, 22, unroll=22)
+    def _(t):
+        q = lax.rem(t, 2)
+        m0 = 6 * (t // 2)
+        at = pl.ds(pl.multiple_of(32 * m0, 64), 256)
+        second(f_hi[q, at, :], f_lo[q, at, :],
+               [(yo, 2 * (m0 + yo) + q - 4, 2 * (yo % 2) + q, m0 // 2 + yo // 2) for yo in range(6)])
+
+    tail = pl.ds(66 * 32, 128)
+    both = lambda f: jnp.concatenate([f[0, tail, :], f[1, tail, :]], axis=0)
+    second(both(f_hi), both(f_lo),
+           [(4 * q + e, 2 * (66 + e) + q - 4, 2 * e + q, 33) for q in range(2) for e in range(2)])
+
     b3 = bias_ref[1]
 
     whole = out_s.reshape(32, 128, 128)
     writes = []
-    for step, (n0, first, count) in enumerate(
-            ((0, 0, 24), (6, 24, 24), (12, 48, 24), (18, 72, 24), (24, 96, 8), (26, 104, 24))):
-        at = pl.ds(32 * n0, 256)
-        for half in range(2):
-            hs, ls, wh, wl = [], [], [], []
-            for dx in range(3):
-                hs.append(jnp.concatenate([s_hi[dx, 2 * half, at, :], s_hi[dx, 2 * half + 1, at, :]], axis=1))
-                ls.append(jnp.concatenate([s_lo[dx, 2 * half, at, :], s_lo[dx, 2 * half + 1, at, :]], axis=1))
-                wh.append(w3_ref[0, dx])
-                wl.append(w3_ref[1, dx])
-            acc = jnp.dot(jnp.concatenate(wh + wl + wh, axis=1), jnp.concatenate(hs + hs + ls, axis=0),
-                          preferred_element_type=F32)
-            for e in range(2):
-                for yo in range(6):
-                    v = acc[yo * 32:yo * 32 + 32, e * 128:e * 128 + 128] + b3
-                    y = 4 * (n0 + yo) + 2 * half + e
-                    for k in range(4):
-                        out_s[pl.ds(k * 1024 + y, 8, stride=128), :] = v[8 * k:8 * k + 8, :]
+    def third(pick_block, places):
+        hs, ls, wh, wl = [], [], [], []
+        for dx in range(3):
+            hs.append(pick_block(s_hi, dx))
+            ls.append(pick_block(s_lo, dx))
+            wh.append(w3_ref[0, dx])
+            wl.append(w3_ref[1, dx])
+        acc = jnp.dot(jnp.concatenate(wh + wl + wh, axis=1), jnp.concatenate(hs + hs + ls, axis=0),
+                      preferred_element_type=F32)
+        for yo, e, y in places:
+            v = acc[yo * 32:yo * 32 + 32, e * 128:e * 128 + 128] + b3
+            for k in range(4):
+                out_s[pl.ds(k * 1024 + y, 8, stride=128), :] = v[8 * k:8 * k + 8, :]
+
+    for step in range(6):
+        first, count = 24 * step, 24
+        if step < 5:
+            at = pl.ds(32 * 6 * step, 256)
+            for half in range(2):
+                third(lambda s, dx: jnp.concatenate([s[dx, 2 * half, at, :], s[dx, 2 * half + 1, at, :]], axis=1),
+                      [(yo, e, 4 * (6 * step + yo) + 2 * half + e) for e in range(2) for yo in range(6)])
+        else:
+            count = 8
+            at = pl.ds(32 * 30, 128)
+            third(lambda s, dx: jnp.concatenate(
+                [jnp.concatenate([s[dx, 2 * half, at, :], s[dx, 2 * half + 1, at, :]], axis=1) for half in range(2)],
+                axis=0),
+                [(4 * half + f, e, 4 * (30 + f) + 2 * half + e)
+                 for half in range(2) for e in range(2) for f in range(2)])
         rows = pl.ds(first, count)
         writes.append(pltpu.make_async_copy(whole.at[:, rows, :], out_ref.at[:, rows, :], out_sem.at[step]))
         writes[-1].start()

time: 34.5 us -> 32.5 us (0.942)
  Pallas kernels: 34.3 us -> 32.4 us
    pallas_call x1, Pallas kernels: 13.6 us -> 11.7 us  [conv_call(): pl.pallas_call(conv_kernel, out_shape=jax.ShapeDtypeStruct((32, 128, 128)...]
where the time goes in v4:
time: 32.5 us; the launch traced here: 32.4 us
  Pallas kernels  32.4 us (100%)
    pallas_call x1, Pallas kernels, comm_call(): pl.pallas_call(comm_kernel, out_shape=[jax.ShapeDtypeStruct((152, 256), F...  20.7 us
    pallas_call x1, Pallas kernels, conv_call(): pl.pallas_call(conv_kernel, out_shape=jax.ShapeDtypeStruct((32, 128, 128)...  11.7 us

profile of v4, /device:TPU:1, one launch (start us, length us, event | category | flops | bytes accessed | tf_op | source)
XLA Modules:
  0.0 32.4 jit_solution(12215274185157477890)
XLA Ops:
  0.0 20.7 %coadd.1 = (f32[152,256]{1,0:T(8,128)S(1)}, bf16[256,256]{1,0:T(8,128)(2,1)S(1)}, bf16[2,3,192,256]{3,2,1,0:T(8,128)(2,1)S(1)}, bf16[2,3,192,256]{3,2,1,0:T(8,128)(2,1)S(1)}, f32[2,32,128]{2,1,0:T(8,128)S(1)}) custom-call(s32[1,8]{1,0:T(1,128)} %bitcast.19, s32[1,8]{1,0:T(1,128)} %bitcast.20, s32[1,8]{1,0:T(1,128)} %bitcast.21, f32[1,8]{1,0:T(1,128)} %bitcast.22, ...), custom_call_target="tpu_custom_call" | custom-call | tf_op jit(solution)/shard_map/coadd/pallas_call | solution.py:354
  20.7 11.7 %convs.1 = f32[32,128,128]{2,1,0:T(8,128)} custom-call(f32[152,256]{1,0:T(8,128)S(1)} %get-tuple-element.10.refs_0_, bf16[256,256]{1,0:T(8,128)(2,1)S(1)} %get-tuple-element.11.refs_1_, bf16[2,3,192,256]{3,2,1,0:T(8,128)(2,1)S(1)} %get-tuple-element.12.refs_2_, bf16[2,3,192,256]{3,2,1,0:T(8,128)(2,1)S(1)} %get-tuple-element.13.refs_3_, ...), custom_call_target="tpu_custom_call" | custom-call | tf_op jit(solution)/shard_map/convs/pallas_call | solution.py:170

commit v5 on v4

--- a/solution.py
+++ b/solution.py
@@ -240,8 +240,7 @@
 
     sub8 = lax.broadcasted_iota(jnp.int32, (8, 128), 0)
 
-    @pl.loop(0, N_COL, unroll=4)
-    def _(c):
+    def fill(c, slot):
         acc = None
         ro = jnp.float32(0.0)
         co = jnp.float32(0.0)
@@ -254,8 +253,8 @@
             w = w + wt
             term = packed[t] * wt
             acc = term if acc is None else acc + term
-        send[c, 0:32, :] = acc
-        send[c, 32:40, :] = jnp.where(sub8 == 0, ro, jnp.where(sub8 == 1, co, w))
+        slot[0:32, :] = acc
+        slot[32:40, :] = jnp.where(sub8 == 0, ro, jnp.where(sub8 == 1, co, w))
 
     pl.semaphore_wait(barrier, N_COL - 1 + 6)
 
@@ -266,9 +265,11 @@
             device_id=(row, c), device_id_type=MESH)
 
     for k in ORDER:
+        c = lax.rem(col + k, N_COL)
+        fill(c, send.at[c])
         tile_copy(k).start()
 
-    recv[0] = send[col]
+    fill(col, recv.at[0])
     for f in fetches[7:]:
         f.wait()
     build_weights(f1, vec, f2, f3, w1_ref, w2_ref, w3_ref, bias_ref)

time: 32.5 us -> 32.7 us (level)
  no operation moved by 1% of the time
where the time goes in v5:
time: 32.7 us; the launch traced here: 32.5 us
  Pallas kernels  32.5 us (99%)
    pallas_call x1, Pallas kernels, comm_call(): pl.pallas_call(comm_kernel, out_shape=[jax.ShapeDtypeStruct((152, 256), F...  20.8 us
    pallas_call x1, Pallas kernels, conv_call(): pl.pallas_call(conv_kernel, out_shape=jax.ShapeDtypeStruct((32, 128, 128)...  11.7 us

profile of v5, /device:TPU:1, one launch (start us, length us, event | category | flops | bytes accessed | tf_op | source)
XLA Modules:
  0.0 32.5 jit_solution(13230694849274832175)
XLA Ops:
  0.0 20.8 %coadd.1 = (f32[152,256]{1,0:T(8,128)S(1)}, bf16[256,256]{1,0:T(8,128)(2,1)S(1)}, bf16[2,3,192,256]{3,2,1,0:T(8,128)(2,1)S(1)}, bf16[2,3,192,256]{3,2,1,0:T(8,128)(2,1)S(1)}, f32[2,32,128]{2,1,0:T(8,128)S(1)}) custom-call(s32[1,8]{1,0:T(1,128)} %bitcast.19, s32[1,8]{1,0:T(1,128)} %bitcast.20, s32[1,8]{1,0:T(1,128)} %bitcast.21, f32[1,8]{1,0:T(1,128)} %bitcast.22, ...), custom_call_target="tpu_custom_call" | custom-call | tf_op jit(solution)/shard_map/coadd/pallas_call | solution.py:355
  20.9 11.7 %convs.1 = f32[32,128,128]{2,1,0:T(8,128)} custom-call(f32[152,256]{1,0:T(8,128)S(1)} %get-tuple-element.10.refs_0_, bf16[256,256]{1,0:T(8,128)(2,1)S(1)} %get-tuple-element.11.refs_1_, bf16[2,3,192,256]{3,2,1,0:T(8,128)(2,1)S(1)} %get-tuple-element.12.refs_2_, bf16[2,3,192,256]{3,2,1,0:T(8,128)(2,1)S(1)} %get-tuple-element.13.refs_3_, ...), custom_call_target="tpu_custom_call" | custom-call | tf_op jit(solution)/shard_map/convs/pallas_call | solution.py:170

commit v6 on v4

--- a/solution.py
+++ b/solution.py
@@ -65,14 +65,15 @@
     base = row * 128
 
     def valid(y):
+        if 0 <= y < 128:
+            return 1.0
         yy = base + y
         return jnp.where(jnp.logical_and(yy >= 0, yy < n_rows), 1.0, 0.0)
 
-    @pl.loop(0, 18, unroll=18)
-    def _(g):
+    for g in range(18):
         hs, ls = [], []
         for dx in range(3):
-            h, l = split(ps[dx, pl.ds(pl.multiple_of(8 * g, 8), 16), :])
+            h, l = split(ps[dx, pl.ds(8 * g, 16), :])
             hs.append(h)
             ls.append(l)
         rhs = jnp.concatenate(hs + ls + hs + [ones, pad], axis=0)
@@ -82,7 +83,7 @@
                 mask = cmask * valid(8 * g + 2 * m + q - 6)
                 v = jnp.maximum(acc[q * 128 + m * 32:q * 128 + m * 32 + 32, :], 0.0) * mask
                 h, l = split(v)
-                at = pl.ds(pl.multiple_of((4 * g + m) * 32, 32), 32)
+                at = pl.ds((4 * g + m) * 32, 32)
                 f_hi[q, at, :] = h
                 f_lo[q, at, :] = l
 
@@ -98,17 +99,16 @@
         for yo, y, r, n in places:
             mask = cmask * valid(y)
             v = jnp.maximum(acc[yo * 32:yo * 32 + 32, :] + b2, 0.0) * mask
-            at = pl.ds(pl.multiple_of(n * 32, 32), 32)
+            at = pl.ds(n * 32, 32)
             for k, sh in enumerate((pltpu.roll(v, 4, 1), v, pltpu.roll(v, 252, 1))):
                 h, l = split(sh[:, :128])
                 s_hi[k, r, at, :] = h
                 s_lo[k, r, at, :] = l
 
-    @pl.loop(0, 22, unroll=22)
-    def _(t):
-        q = lax.rem(t, 2)
+    for t in range(22):
+        q = t % 2
         m0 = 6 * (t // 2)
-        at = pl.ds(pl.multiple_of(32 * m0, 64), 256)
+        at = pl.ds(32 * m0, 256)
         second(f_hi[q, at, :], f_lo[q, at, :],
                [(yo, 2 * (m0 + yo) + q - 4, 2 * (yo % 2) + q, m0 // 2 + yo // 2) for yo in range(6)])
 
@@ -198,11 +198,17 @@
                 p_ref, w1_ref, w2_ref, w3_ref, bias_ref,
                 dest, roff, coff, wgt, tiles, rker, ckpad, f1, vec, f2, f3, packed, send, recv, spread, pick,
                 edge_out, edge_in, in_sem, send_sem, recv_sem, esend_sem, erecv_sem):
-    fetches = [pltpu.make_async_copy(src, dst, in_sem.at[i]) for i, (src, dst) in enumerate((
-        (rker_h, rker), (tiles_h, tiles), (cker_h, ckpad.at[:, pl.ds(TS, TS), :]), (coff_h, coff),
-        (dest_h, dest), (roff_h, roff), (wgt_h, wgt), (f2_h, f2), (f3_h, f3),
-        (f1_h, f1), (b1_h, vec.at[0]), (b2_h, vec.at[1]), (b3_h, vec.at[2])))]
-    for f in fetches:
+    half = TILES_DEV // 2
+    pairs = []
+    for h in range(2):
+        part = pl.ds(h * half, half)
+        pairs += [(rker_h.at[part], rker.at[part]), (tiles_h.at[part], tiles.at[part])]
+        if h == 0:
+            pairs += [(cker_h, ckpad.at[:, pl.ds(TS, TS), :]), (coff_h, coff)]
+    pairs += [(dest_h, dest), (roff_h, roff), (wgt_h, wgt), (f2_h, f2), (f3_h, f3),
+              (f1_h, f1), (b1_h, vec.at[0]), (b2_h, vec.at[1]), (b3_h, vec.at[2])]
+    fetches = [pltpu.make_async_copy(src, dst, in_sem.at[i]) for i, (src, dst) in enumerate(pairs)]
+    for f in fetches[:9]:
         f.start()
     row = lax.axis_index("row")
     col = lax.axis_index("col")
@@ -221,12 +227,15 @@
         for c in (left, col, right):
             pl.semaphore_signal(barrier, inc=1, device_id=(r, c), device_id_type=MESH)
 
+    for f in fetches[9:]:
+        f.start()
     blank = jnp.zeros((TILES_DEV, TS, TS), F32)
     ckpad[:, 0:TS, :] = blank
     ckpad[:, 2 * TS:3 * TS, :] = blank
-    for f in fetches[:4]:
-        f.wait()
     for t in range(TILES_DEV):
+        if t % half == 0:
+            for f in fetches[:4] if t == 0 else fetches[4:6]:
+                f.wait()
         rh, rl = split(rker[t])
         th, tl = split(tiles[t])
         mid = dot3(rh, rl, th, tl, ((1,), (0,)))
@@ -235,7 +244,7 @@
         ch, cl = split(placed)
         img = dot3(mh, ml, ch, cl, ((1,), (1,)))
         packed[t] = img[:32, :] + pltpu.roll(img[32:, :], 64, 1)
-    for f in fetches[4:7]:
+    for f in fetches[6:9]:
         f.wait()
 
     sub8 = lax.broadcasted_iota(jnp.int32, (8, 128), 0)
@@ -269,7 +278,7 @@
         tile_copy(k).start()
 
     recv[0] = send[col]
-    for f in fetches[7:]:
+    for f in fetches[9:]:
         f.wait()
     build_weights(f1, vec, f2, f3, w1_ref, w2_ref, w3_ref, bias_ref)
 
@@ -375,7 +384,7 @@
             pltpu.VMEM((128, N_COL * TS), BF),
             pltpu.VMEM((4, 8, 128), F32),
             pltpu.VMEM((8, 8, 128), F32),
-            pltpu.SemaphoreType.DMA((13,)),
+            pltpu.SemaphoreType.DMA((15,)),
             pltpu.SemaphoreType.DMA((N_COL,)),
             pltpu.SemaphoreType.DMA((N_COL,)),
             pltpu.SemaphoreType.DMA((8,)),

time: 32.5 us -> 32.4 us (level)
  no operation moved by 1% of the time
where the time goes in v6:
time: 32.4 us; the launch traced here: 32.3 us
  Pallas kernels  32.3 us (100%)
    pallas_call x1, Pallas kernels, comm_call(): pl.pallas_call(comm_kernel, out_shape=[jax.ShapeDtypeStruct((152, 256), F...  20.7 us
    pallas_call x1, Pallas kernels, conv_call(): pl.pallas_call(conv_kernel, out_shape=jax.ShapeDtypeStruct((32, 128, 128)...  11.6 us

profile of v6, /device:TPU:1, one launch (start us, length us, event | category | flops | bytes accessed | tf_op | source)
XLA Modules:
  0.0 32.3 jit_solution(15185348700173388134)
XLA Ops:
  0.0 20.7 %coadd.1 = (f32[152,256]{1,0:T(8,128)S(1)}, bf16[256,256]{1,0:T(8,128)(2,1)S(1)}, bf16[2,3,192,256]{3,2,1,0:T(8,128)(2,1)S(1)}, bf16[2,3,192,256]{3,2,1,0:T(8,128)(2,1)S(1)}, f32[2,32,128]{2,1,0:T(8,128)S(1)}) custom-call(s32[1,8]{1,0:T(1,128)} %bitcast.19, s32[1,8]{1,0:T(1,128)} %bitcast.20, s32[1,8]{1,0:T(1,128)} %bitcast.21, f32[1,8]{1,0:T(1,128)} %bitcast.22, ...), custom_call_target="tpu_custom_call" | custom-call | tf_op jit(solution)/shard_map/coadd/pallas_call | solution.py:363
  20.7 11.6 %convs.1 = f32[32,128,128]{2,1,0:T(8,128)} custom-call(f32[152,256]{1,0:T(8,128)S(1)} %get-tuple-element.10.refs_0_, bf16[256,256]{1,0:T(8,128)(2,1)S(1)} %get-tuple-element.11.refs_1_, bf16[2,3,192,256]{3,2,1,0:T(8,128)(2,1)S(1)} %get-tuple-element.12.refs_2_, bf16[2,3,192,256]{3,2,1,0:T(8,128)(2,1)S(1)} %get-tuple-element.13.refs_3_, ...), custom_call_target="tpu_custom_call" | custom-call | tf_op jit(solution)/shard_map/convs/pallas_call | solution.py:170
